TPU v7x, 128 devices: a whole 4x4x4 slice. The times are simulated.
128 devices in a mesh: row: 8 (over x, z_lo), col: 16 (over z_hi, y, core).
Axes of the slice: x: 4, y: 4, z: 4 (z_hi: 2, z_lo: 2; z = z_hi * 2 + z_lo), core: 2. Of those that a mesh axis runs over, the one named last changes fastest.
Arguments:
- image: bfloat16 [128, 512, 768], P('row', 'col'), may hold values from -6 to 6
- conv_taps: float32 [9, 768], replicated, may hold values from -0.5 to 0.5
- w_query: bfloat16 [768, 768], replicated, may hold values from -0.21875 to 0.21875
- w_key: bfloat16 [768, 768], replicated, may hold values from -0.21875 to 0.21875
- w_value: bfloat16 [768, 768], replicated, may hold values from -0.21875 to 0.21875
- w_out: bfloat16 [768, 768], replicated, may hold values from -0.21875 to 0.21875
- grad_out: bfloat16 [128, 512, 768], P('row', 'col'), may hold values from -6 to 6
Outputs:
- grad_image: bfloat16 [128, 512, 768], P('row', 'col')
- grad_weights: float32 [768, 3072], P(None, 'col')
- grad_conv: float32 [9, 768], P(None, 'col')
All inputs are finite; a program needn't handle non-finite values.
Results may differ from a plain program's by a relative error of at most 0.022.
Values may be sent and summed in bfloat16 or wider, within the bound.
No kernel may reach another device: no remote copies, remote signals or barrier semaphores. Data moves between devices by JAX's collectives and lax.ppermute only.
A program may use at most 128 MiB of HBM per device.

v0:
```python
import jax
import jax.numpy as jnp
from jax import lax
from jax.experimental import pallas as pl
from jax.experimental.pallas import tpu as pltpu
from jax.sharding import PartitionSpec as P

HD = 64
POOL = 8
EPSILON = 1e-05
BF = jnp.bfloat16
F32 = jnp.float32
LANES = 128
WIDE = 256

FINAL = (0, 1, 2, 3, 12, 13, 14, 15)
PARTNER = (5, 4, 7, 6, 9, 8, 11, 10)
SLICE_AT = tuple((FINAL.index(j) if j in FINAL else PARTNER.index(j)) for j in range(16))
PAIRS = [(j, j ^ 1) for j in range(16)]
BOTH = ("row", "col")


def holder(piece, core):
    return FINAL[piece] if FINAL[piece] % 2 == core else PARTNER[piece]


SUM_GROUPS = [[q * 16 + holder(s, c) for s in range(8) for q in range(8)] for c in range(2)]
PLACE_GROUPS = [[q * 16 + holder(s, c) for c in range(2) for q in range(8)] for s in range(8)]


def from_both_sides(first, last, axis):
    count = lax.axis_size(axis)
    before = lax.ppermute(last, axis, [(i, (i + 1) % count) for i in range(count)])
    after = lax.ppermute(first, axis, [((i + 1) % count, i) for i in range(count)])
    return before, after


def edges_of(tile, is_first, is_last):
    top, bottom = from_both_sides(tile[0], tile[-1], "row")
    up = jnp.where(is_first, 0, top).astype(BF)
    down = jnp.where(is_last, 0, bottom).astype(BF)
    first = jnp.concatenate([up[:1], tile[:, 0], down[:1]], axis=0)
    last = jnp.concatenate([up[-1:], tile[:, -1], down[-1:]], axis=0)
    left, right = from_both_sides(first, last, "col")
    return top, bottom, left, right


def dot(left, right, dims):
    return lax.dot_general(left, right, ((dims[0], dims[1]), ((), ())), preferred_element_type=F32)


def contract_first(left, right):
    return dot(left, right, ((0,), (0,)))


def contract_last(left, right):
    return dot(left, right, ((1,), (1,)))


def put_sides(padded, flags, top, bottom, left, right):
    padded[0, 8:40, :] = top[...].astype(F32) * flags[0].astype(F32)
    padded[17, 8:40, :] = bottom[...].astype(F32) * flags[1].astype(F32)
    first = left[...].astype(F32) * flags[2].astype(F32)
    last = right[...].astype(F32) * flags[3].astype(F32)
    for row in range(18):
        padded[row, 7:8, :] = first[row : row + 1]
        padded[row, 40:41, :] = last[row : row + 1]


def windows_of(padded, at):
    kept = {}

    def window(row, shift):
        if (row, shift) not in kept:
            kept[row, shift] = padded[row, 7 + shift : 39 + shift, at]
        return kept[row, shift]

    return window


def mix_kernel(
    flags, image, top, bottom, left, right, taps, hidden, standard, inverse, normed, padded, pools
):
    step = pl.program_id(0)
    put_sides(padded, flags, top, bottom, left, right)
    padded[1:17, 8:40, :] = image[...].astype(F32)
    per = WIDE // LANES
    for part in range(per):
        at = slice(part * LANES, (part + 1) * LANES)
        weights = taps[:, at]
        window = windows_of(padded, at)
        for cell_row in range(2):
            column = jnp.zeros((32, LANES), F32)
            for row in range(cell_row * POOL, (cell_row + 1) * POOL):
                total = window(row + 1, 1)
                for a in range(3):
                    for b in range(3):
                        tap = 3 * a + b
                        total = total + weights[tap : tap + 1] * window(row + a, b)
                rounded = total.astype(BF)
                hidden[row * 32 : (row + 1) * 32, at] = rounded
                column = column + rounded.astype(F32)
            for cell in range(4):
                one = jnp.sum(column[cell * POOL : (cell + 1) * POOL], axis=0, keepdims=True)
                place = 4 * cell_row + cell
                pools[step * per + part, place : place + 1, :] = one * (1.0 / (POOL * POOL))

    @pl.when(step == pl.num_programs(0) - 1)
    def _():
        blocks = pools.shape[0]
        scale = 1.0 / (blocks * LANES)
        pooled = [pools[i] for i in range(blocks)]
        centre = sum(jnp.sum(x, axis=1, keepdims=True) for x in pooled) * scale
        moved = [x - centre for x in pooled]
        spread = sum(jnp.sum(x * x, axis=1, keepdims=True) for x in moved) * scale
        factor = lax.rsqrt(spread + EPSILON)
        inverse[...] = jnp.broadcast_to(factor, inverse.shape)
        for i in range(blocks):
            at = slice(i * LANES, (i + 1) * LANES)
            own = moved[i] * factor
            standard[:, at] = own
            normed[:, :, at] = jnp.broadcast_to(own.astype(BF)[None], (16, 8, LANES))


def side_specs():
    return [
        pl.BlockSpec((32, WIDE), lambda i: (0, i)),
        pl.BlockSpec((32, WIDE), lambda i: (0, i)),
        pl.BlockSpec((18, WIDE), lambda i: (0, i)),
        pl.BlockSpec((18, WIDE), lambda i: (0, i)),
    ]


SCALARS = pl.BlockSpec(memory_space=pltpu.SMEM)


def mix(flags, image, sides, taps):
    height, width, channels = image.shape
    return pl.pallas_call(
        mix_kernel,
        grid=(channels // WIDE,),
        in_specs=[
            SCALARS,
            pl.BlockSpec((height, width, WIDE), lambda i: (0, 0, i)),
            *side_specs(),
            pl.BlockSpec((9, WIDE), lambda i: (0, i)),
        ],
        out_specs=[
            pl.BlockSpec((height * width, WIDE), lambda i: (0, i)),
            pl.BlockSpec((8, channels), lambda i: (0, 0)),
            pl.BlockSpec((8, LANES), lambda i: (0, 0)),
            pl.BlockSpec((16, 8, channels), lambda i: (0, 0, 0)),
        ],
        out_shape=[
            jax.ShapeDtypeStruct((height * width, channels), BF),
            jax.ShapeDtypeStruct((8, channels), F32),
            jax.ShapeDtypeStruct((8, LANES), F32),
            jax.ShapeDtypeStruct((16, 8, channels), BF),
        ],
        scratch_shapes=[
            pltpu.VMEM((18, 48, WIDE), F32),
            pltpu.VMEM((channels // LANES, 8, LANES), F32),
        ],
        cost_estimate=pl.CostEstimate(flops=8_000_000, bytes_accessed=2_000_000, transcendentals=0),
        name="mix",
    )(flags, image, *sides, taps)


def attend_kernel(query, dout, cells, w_key, w_value, attended, grad_query, sums):
    low = lax.broadcasted_iota(jnp.int32, (128, LANES), 1) < HD
    all_cells = cells[...]
    zero = jnp.zeros((128, LANES), BF)

    def two_heads(weight):
        both = jnp.dot(all_cells, weight[...], preferred_element_type=F32).astype(BF)
        return jnp.concatenate([jnp.where(low, both, zero), jnp.where(low, zero, both)], axis=0)

    keys = two_heads(w_key) * jnp.asarray(HD**-0.5, BF)
    values = two_heads(w_value)
    q, d = query[...], dout[...]
    expons = jnp.exp(contract_last(keys, q))
    grads = contract_last(values, d)
    probs, scores = [], []
    for head in range(2):
        own = expons[head * 128 : (head + 1) * 128]
        prob = own * (1.0 / jnp.sum(own, axis=0, keepdims=True))
        grad = grads[head * 128 : (head + 1) * 128]
        delta = jnp.sum(prob * grad, axis=0, keepdims=True)
        probs.append(prob.astype(BF))
        scores.append((prob * (grad - delta)).astype(BF))
    weights = jnp.concatenate(probs, axis=0)
    grad_scores = jnp.concatenate(scores, axis=0)
    attended[...] = contract_first(values, weights).astype(BF)
    grad_query[...] = contract_first(keys, grad_scores).astype(BF)
    grad_keys = jnp.dot(grad_scores, q, preferred_element_type=F32)
    grad_values = jnp.dot(weights, d, preferred_element_type=F32)
    grad_keys = jnp.where(low, grad_keys[:128], grad_keys[128:]) * (HD**-0.5)
    grad_values = jnp.where(low, grad_values[:128], grad_values[128:])
    sums[:, 0] = grad_keys.astype(BF).reshape(16, 8, LANES)
    sums[:, 1] = grad_values.astype(BF).reshape(16, 8, LANES)


def attend(query, dout, cells, w_key, w_value):
    tokens, channels = query.shape
    by_pair = pl.BlockSpec((tokens, LANES), lambda i: (0, i))
    turned = pl.BlockSpec((LANES, tokens), lambda i: (i, 0))
    weight = pl.BlockSpec((channels, LANES), lambda i: (0, i))
    return pl.pallas_call(
        attend_kernel,
        grid=(channels // LANES,),
        in_specs=[
            by_pair,
            by_pair,
            pl.BlockSpec((128, channels), lambda i: (0, 0)),
            weight,
            weight,
        ],
        out_specs=[turned, turned, pl.BlockSpec((16, 2, 8, LANES), lambda i: (0, 0, 0, i))],
        out_shape=[
            jax.ShapeDtypeStruct((channels, tokens), BF),
            jax.ShapeDtypeStruct((channels, tokens), BF),
            jax.ShapeDtypeStruct((16, 2, 8, channels), BF),
        ],
        cost_estimate=pl.CostEstimate(
            flops=3_000_000_000, bytes_accessed=6_000_000, transcendentals=800_000
        ),
        name="attend",
    )(query, dout, cells, w_key, w_value)


def taps_kernel(flags, image, top, bottom, left, right, early, terms, windows, padded, lines):
    put_sides(padded, flags, top, bottom, left, right)
    padded[1:17, 8:40, :] = image[...].astype(F32)
    for part in range(WIDE // LANES):
        at = slice(part * LANES, (part + 1) * LANES)
        window = windows_of(padded, at)
        totals = [jnp.zeros((8, LANES), F32) for _ in range(9)]
        for row in range(16):
            grad = early[row, :, at]
            for a in range(3):
                for b in range(3):
                    term = grad * window(row + a, b)
                    totals[3 * a + b] = totals[3 * a + b] + (
                        (term[:8] + term[8:16]) + (term[16:24] + term[24:])
                    )
        for tap in range(9):
            terms[tap : tap + 1, at] = jnp.sum(totals[tap], axis=0, keepdims=True)
    for cell_row in range(2):
        for a in range(3):
            start = cell_row * POOL + a
            line = padded[start]
            for row in range(start + 1, start + POOL):
                line = line + padded[row]
            lines[...] = line
            for b in range(3):
                for cell in range(4):
                    part = lines[7 + b + 8 * cell : 15 + b + 8 * cell, :]
                    place = 4 * cell_row + cell
                    windows[3 * a + b, place : place + 1, :] = jnp.sum(part, axis=0, keepdims=True)


def tap_terms(flags, image, sides, early):
    height, width, channels = image.shape
    block = pl.BlockSpec((height, width, WIDE), lambda i: (0, 0, i))
    return pl.pallas_call(
        taps_kernel,
        grid=(channels // WIDE,),
        in_specs=[SCALARS, block, *side_specs(), block],
        out_specs=[
            pl.BlockSpec((9, WIDE), lambda i: (0, i)),
            pl.BlockSpec((9, 8, WIDE), lambda i: (0, 0, i)),
        ],
        out_shape=[
            jax.ShapeDtypeStruct((9, channels), F32),
            jax.ShapeDtypeStruct((9, 8, channels), F32),
        ],
        scratch_shapes=[pltpu.VMEM((18, 48, WIDE), F32), pltpu.VMEM((48, WIDE), F32)],
        cost_estimate=pl.CostEstimate(flops=8_000_000, bytes_accessed=3_000_000, transcendentals=0),
        name="tap_terms",
    )(flags, image, *sides, early)


def window_of(x, start):
    base = min(start // LANES * LANES, x.shape[1] - 2 * LANES)
    if start == base:
        return x[:, base : base + LANES]
    return pltpu.roll(x[:, base : base + 2 * LANES], base - start + 2 * LANES, 1)[:, :LANES]


def cells_kernel(terms, w_key, w_value, standard, inverse, early, windows, grad_pooled, blocks):
    received = jnp.sum(terms[...].astype(F32), axis=0)
    keys, values = received[0], received[1]
    grad = contract_last(keys.astype(BF), w_key[...]) + contract_last(values.astype(BF), w_value[...])
    own = standard[...]
    scale = 1.0 / own.shape[1]
    centre = jnp.sum(grad, axis=1, keepdims=True) * scale
    along = jnp.sum(grad * own, axis=1, keepdims=True) * scale
    pooled = (grad - centre - own * along) * (inverse[:, :1] * (1.0 / (POOL * POOL)))
    grad_pooled[...] = pooled
    conv = [
        early[t : t + 1, :] + jnp.sum(pooled * windows[t], axis=0, keepdims=True) for t in range(9)
    ]
    first, last = jnp.concatenate(conv[:8], axis=0), jnp.broadcast_to(conv[8], (8, own.shape[1]))
    lane = lax.broadcasted_iota(jnp.int32, (8, LANES), 1)
    both = jnp.concatenate([keys, values], axis=1)
    width = own.shape[1] // 16
    pieces = {}
    for j in range(16):
        part = PARTNER[SLICE_AT[j]] - 4
        taps = pltpu.roll(window_of(first, width * j), 24, 1)
        tail = pltpu.roll(window_of(last, width * j), 72, 1)
        rest = jnp.where(lane < 72, taps, tail)
        for q in range(8):
            if (part, q) not in pieces:
                pieces[part, q] = window_of(both, 192 * part + 24 * q)
            blocks[16 * q + j] = jnp.where(lane < 24, pieces[part, q], rest).astype(BF)


def at_cells(terms, w_key, w_value, standard, inverse, early, windows):
    channels = standard.shape[1]
    return pl.pallas_call(
        cells_kernel,
        out_shape=[
            jax.ShapeDtypeStruct((8, channels), F32),
            jax.ShapeDtypeStruct((128, 8, LANES), BF),
        ],
        cost_estimate=pl.CostEstimate(flops=30_000_000, bytes_accessed=3_500_000, transcendentals=0),
        name="at_cells",
    )(terms, w_key, w_value, standard, inverse, early, windows)


def pieces_kernel(flags, got, blocks, near, far, placed, conv):
    piece = jnp.sum(got[...].astype(F32), axis=0).astype(BF)
    conv[...] = jnp.sum(blocks[...].astype(F32), axis=0)
    total = jnp.zeros((LANES, piece.shape[1]), F32)
    for i in range(8):
        row = jnp.bitwise_xor(flags[5], i)
        own = blocks[pl.ds(row * 16, 16)].reshape(128, LANES)
        total = total + contract_first(own, near[i] if i < 4 else far[i - 4])
    cell_piece = total[:24].astype(BF)
    odd = flags[4] == 1
    first = jnp.where(odd, cell_piece, piece)
    second = jnp.where(odd, piece, cell_piece)
    for q in range(8):
        placed[q] = first
        placed[8 + q] = second


def pieces(flags, got, blocks, near, far):
    half = near.shape[2]
    vmem = pl.BlockSpec(memory_space=pltpu.VMEM)
    return pl.pallas_call(
        pieces_kernel,
        in_specs=[SCALARS, vmem, vmem, vmem, vmem],
        out_shape=[
            jax.ShapeDtypeStruct((16, 24, half), BF),
            jax.ShapeDtypeStruct((8, LANES), F32),
        ],
        cost_estimate=pl.CostEstimate(flops=100_000_000, bytes_accessed=2_500_000, transcendentals=0),
        name="pieces",
    )(flags, got, blocks, near, far)


def unmix_kernel(flags, early, pooled, top, bottom, left, right, taps, image, padded):
    put_sides(padded, flags, top, bottom, left, right)
    for row in range(16):
        for cell in range(4):
            place = 4 * (row // POOL) + cell
            at = slice(8 * cell, 8 * cell + 8)
            padded[row + 1, 8 + 8 * cell : 16 + 8 * cell, :] = (
                early[row, at, :] + pooled[place : place + 1, :]
            )
    for part in range(WIDE // LANES):
        at = slice(part * LANES, (part + 1) * LANES)
        weights = taps[:, at]
        window = windows_of(padded, at)
        for row in range(16):
            total = window(row + 1, 1)
            for a in range(3):
                for b in range(3):
                    tap = 3 * a + b
                    total = total + weights[tap : tap + 1] * window(row + 2 - a, 2 - b)
            image[row, :, at] = total.astype(BF)


def unmix(flags, early, pooled, sides, taps):
    height, width, channels = early.shape
    block = pl.BlockSpec((height, width, WIDE), lambda i: (0, 0, i))
    return pl.pallas_call(
        unmix_kernel,
        grid=(channels // WIDE,),
        in_specs=[
            SCALARS,
            block,
            pl.BlockSpec((8, WIDE), lambda i: (0, i)),
            *side_specs(),
            pl.BlockSpec((9, WIDE), lambda i: (0, i)),
        ],
        out_specs=block,
        out_shape=jax.ShapeDtypeStruct((height, width, channels), BF),
        scratch_shapes=[pltpu.VMEM((18, 48, WIDE), F32)],
        cost_estimate=pl.CostEstimate(flops=8_000_000, bytes_accessed=3_000_000, transcendentals=0),
        name="unmix",
    )(flags, early, pooled, *sides, taps)


def block_gradients(image, conv_taps, w_query, w_key, w_value, w_out, grad_out):
    height, width, channels = image.shape
    half = channels // 2
    at_row, at_col = lax.axis_index("row"), lax.axis_index("col")
    core = at_col % 2
    is_first, is_last = at_row == 0, at_row == lax.axis_size("row") - 1
    turned = (core == 1) ^ ((at_col >= 4) & (at_col < 12))
    flags = jnp.stack(
        [
            ~is_first,
            ~is_last,
            at_col > 0,
            at_col < lax.axis_size("col") - 1,
            turned,
        ]
    ).astype(jnp.int32)
    flags = jnp.concatenate([flags, at_row[None].astype(jnp.int32)])
    flat_grad = grad_out.reshape(-1, channels)
    sides = edges_of(image, is_first, is_last)
    dout = contract_last(flat_grad, w_out).astype(BF)
    hidden, standard, inverse, normed = mix(flags, image, sides, conv_taps)
    cells = lax.all_to_all(normed, "col", 0, 0, tiled=True)
    cells = cells.reshape(-1, channels)
    query = jnp.dot(hidden, w_query, preferred_element_type=F32).astype(BF)
    near = lax.dynamic_slice_in_dim(cells, core * half, half, axis=1)[None]
    for step in range(3):
        far = lax.ppermute(near, "row", [(i, i ^ (1 << step)) for i in range(8)])
        if step < 2:
            near = jnp.concatenate([near, far], axis=0)
    attended, grad_query, sums = attend(query, dout, cells, w_key, w_value)
    terms = lax.all_to_all(sums, "col", 0, 0, tiled=True)

    def half_terms(which):
        h = lax.dynamic_slice_in_dim(hidden, which * half, half, axis=1)
        a = lax.dynamic_slice_in_dim(attended, which * half, half, axis=0)
        return (
            dot(grad_query, h, ((1,), (0,))).astype(BF),
            dot(flat_grad, a, ((0,), (1,))).astype(BF),
        )

    sent = half_terms(1 - core)
    theirs = [lax.ppermute(x, "col", PAIRS) for x in sent]
    own = lax.optimization_barrier(half_terms(core))
    chip = jnp.concatenate(
        [x.astype(F32) + y.astype(F32) for x, y in zip(own, theirs)], axis=0
    ).astype(BF)
    chip, terms = lax.optimization_barrier((chip, terms))
    got = lax.all_to_all(
        chip.reshape(64, 24, half), BOTH, 0, 0, tiled=True, axis_index_groups=SUM_GROUPS
    )
    grad_hidden = dot(grad_query, w_query, ((0,), (1,)))
    early = (flat_grad.astype(F32) + grad_hidden).reshape(height, width, channels)
    early_terms, windows = tap_terms(flags, image, sides, early)
    pooled, block = at_cells(
        terms, w_key, w_value, standard, inverse, early_terms, windows
    )
    block, got = lax.optimization_barrier((block, got))
    blocks = lax.all_to_all(block, BOTH, 0, 0, tiled=True)
    rows = jnp.repeat(pooled, POOL, axis=0).reshape(2, width, channels)
    up = jnp.concatenate([pooled[0:1], pooled[4:5]], axis=0)
    down = jnp.concatenate([pooled[3:4], pooled[7:8]], axis=0)
    top, bottom = from_both_sides(
        (early[0] + rows[0]).astype(BF), (early[-1] + rows[1]).astype(BF), "row"
    )
    first = (early[:, 0] + jnp.repeat(up, POOL, axis=0)).astype(BF)
    last = (early[:, -1] + jnp.repeat(down, POOL, axis=0)).astype(BF)
    over = jnp.where(is_first, 0, top).astype(BF)
    under = jnp.where(is_last, 0, bottom).astype(BF)
    left, right = from_both_sides(
        jnp.concatenate([over[:1], first, under[:1]], axis=0),
        jnp.concatenate([over[-1:], last, under[-1:]], axis=0),
        "col",
    )
    grad_image = unmix(flags, early, pooled, (top, bottom, left, right), conv_taps)
    placed, conv = pieces(flags, got, blocks, near, far)
    placed = lax.all_to_all(
        placed, BOTH, 0, 0, tiled=True, axis_index_groups=PLACE_GROUPS
    )
    grad_weights = jnp.transpose(placed.reshape(2, 192, half), (0, 2, 1)).reshape(channels, 192)
    grad_conv = jnp.concatenate([conv[:, 24:72], conv[:1, 72:120]], axis=0)
    return (grad_image, grad_weights.astype(F32), grad_conv)


def solution(mesh):
    return jax.shard_map(
        block_gradients,
        mesh=mesh,
        in_specs=(P("row", "col", None), P(), P(), P(), P(), P(), P("row", "col", None)),
        out_specs=(P("row", "col", None), P(None, "col"), P(None, "col")),
        check_vma=False,
    )
```

profile of v0, /device:TPU:96, one launch (start us, length us, event | category | flops | bytes accessed | tf_op | source)
XLA Modules:
  0.0 146.9 jit_solution(10491784884849811529)
XLA Ops:
  1.6 1.4 collective-permute-start
  3.6 3.2 %convolution_convert_fusion.dout = bf16[512,768]{1,0:T(8,128)(2,1)} fusion(bf16[512,768]{1,0:T(8,128)(2,1)} %bitcast.67, bf16[768,768]{1,0:T(8,128)(2,1)} %param.12), kind=kOutput, calls=%fused_computation.1 | convolution fusion | flops 604372992 | bytes 2752512 | tf_op jit(solution)/shard_map/dot_general | solution.py:49
  8.3 1.9 %collective-permute-start.3 = (bf16[18,768]{1,0:T(8,128)(2,1)S(1)}, bf16[18,768]{1,0:T(8,128)(2,1)S(1)}, u32[]{:S(2)}, u32[]{:S(2)}) collective-permute-start(bf16[18,768]{1,0:T(8,128)(2,1)S(1)} %pad_maximum_fusion.4), channel_id=1, source_target_pairs={{1,0},{2,1},{3,2},{4,3},{5,4},{6,5},{7,6},{8,7},{9,8},{10,9},{11,1... | collective-permute-start | bytes 82952 | tf_op jit(solution)/shard_map/ppermute | solution.py:34
  11.9 5.4 %collective-permute-done.2.left = bf16[18,768]{1,0:T(8,128)(2,1)S(1)} collective-permute-done((bf16[18,768]{1,0:T(8,128)(2,1)S(1)}, bf16[18,768]{1,0:T(8,128)(2,1)S(1)}, u32[]{:S(2)}, u32[]{:S(2)}) %collective-permute-start.2) | collective-permute-done | bytes 27680 | tf_op jit(solution)/shard_map/ppermute | solution.py:33
  17.9 4.5 %mix.1 = (bf16[512,768]{1,0:T(8,128)(2,1)}, f32[8,768]{1,0:T(8,128)}, f32[8,128]{1,0:T(8,128)}, bf16[16,8,768]{2,1,0:T(8,128)(2,1)}) custom-call(s32[6]{0:T(128)} %pad_add_fusion.flags, bf16[16,32,768]{2,1,0:T(8,128)(2,1)} %image.3, bf16[32,768]{1,0:T(8,128)(2,1)} %copy-done.9, bf16[32,768]{1,0:T(8,128)(2,1)} %copy-done.10, bf16[18,768]{1,0:T(8,128)(2,1)} %copy-done.17, ...), custom_call_target="tpu_custom_call" | custom-call | flops 8000000 | bytes 2000000 | tf_op jit(solution)/shard_map/mix/pallas_call | solution.py:139
  22.4 6.3 %all-to-all-start = ((bf16[16,8,768]{2,1,0:T(8,128)(2,1)}), bf16[16,8,768]{2,1,0:T(8,128)(2,1)S(1)}, u32[]{:S(2)}, u32[]{:S(2)}) async-start(bf16[16,8,768]{2,1,0:T(8,128)(2,1)} %get-tuple-element.23), calls=%async_computation | async-start | bytes 393216 | tf_op jit(solution)/shard_map/all_to_all | solution.py:428
  28.8 2.8 %convolution_convert_fusion.1.query = bf16[512,768]{1,0:T(8,128)(2,1)} fusion(bf16[512,768]{1,0:T(8,128)(2,1)} %get-tuple-element.22, bf16[768,768]{1,0:T(8,128)(2,1)S(1)} %copy-done), kind=kOutput, calls=%fused_computation.2 | convolution fusion | flops 604372992 | bytes 2752512 | tf_op jit(solution)/shard_map/dot_general | solution.py:430
  31.6 2.9 %all-to-all-done = bf16[16,8,768]{2,1,0:T(8,128)(2,1)S(1)} async-done(((bf16[16,8,768]{2,1,0:T(8,128)(2,1)}), bf16[16,8,768]{2,1,0:T(8,128)(2,1)S(1)}, u32[]{:S(2)}, u32[]{:S(2)}) %all-to-all-start) | async-done | bytes 196640 | tf_op jit(solution)/shard_map/all_to_all | solution.py:428
  35.1 8.0 %attend.1 = (bf16[768,512]{1,0:T(8,128)(2,1)}, bf16[768,512]{1,0:T(8,128)(2,1)}, bf16[16,2,8,768]{3,2,1,0:T(8,128)(2,1)}) custom-call(bf16[512,768]{1,0:T(8,128)(2,1)} %convolution_convert_fusion.1.query, bf16[512,768]{1,0:T(8,128)(2,1)} %convolution_convert_fusion.dout, bf16[128,768]{1,0:T(8,128)(2,1)} %bitcast.73, bf16[768,768]{1,0:T(8,128)(2,1)} %w_key.3, ...), custom_call_target="tpu_custom_call" | custom-call | flops 3000000000 | bytes 6000000 | tf_op jit(solution)/shard_map/attend/pallas_call | solution.py:208
  43.1 3.2 %convert_add_fusion = f32[512,768]{1,0:T(8,128)} fusion(bf16[512,768]{1,0:T(8,128)(2,1)S(1)} %bitcast.68, bf16[768,512]{1,0:T(8,128)(2,1)} %get-tuple-element.24, bf16[768,768]{1,0:T(8,128)(2,1)S(1)} %copy-done), kind=kOutput, calls=%fused_computation | convolution fusion | flops 604766208 | bytes 4325376 | tf_op jit(solution)/shard_map/dot_general | solution.py:49
  48.3 1.4 convolution_convert_fusion.3
  50.0 2.6 %collective-permute-start.10 = (bf16[1,128,384]{2,1,0:T(8,128)(2,1)S(1)}, bf16[1,128,384]{2,1,0:T(8,128)(2,1)S(1)}, u32[]{:S(2)}, u32[]{:S(2)}) collective-permute-start(bf16[1,128,384]{2,1,0:T(8,128)(2,1)S(1)} %dynamic-slice_bitcast_fusion), channel_id=1, source_target_pairs={{0,16},{16,0},{32,48},{48,32},{64,80},{80,64},{96,112},{112,96},{1... | collective-permute-start | bytes 294920 | tf_op jit(solution)/shard_map/ppermute | solution.py:433
  52.5 1.4 fusion.1
  53.9 7.6 %all-to-all-start.1 = ((bf16[16,2,8,768]{3,2,1,0:T(8,128)(2,1)}), bf16[16,2,8,768]{3,2,1,0:T(8,128)(2,1)}, u32[]{:S(2)}, u32[]{:S(2)}) async-start(bf16[16,2,8,768]{3,2,1,0:T(8,128)(2,1)} %get-tuple-element.28), calls=%async_computation.1 | async-start | bytes 786432 | tf_op jit(solution)/shard_map/all_to_all | solution.py:437
  61.5 4.5 %tap_terms.1 = (f32[9,768]{1,0:T(8,128)}, f32[9,8,768]{2,1,0:T(8,128)}) custom-call(s32[6]{0:T(128)} %pad_add_fusion.flags, bf16[16,32,768]{2,1,0:T(8,128)(2,1)} %image.3, bf16[32,768]{1,0:T(8,128)(2,1)} %copy-done.9, bf16[32,768]{1,0:T(8,128)(2,1)} %copy-done.10, bf16[18,768]{1,0:T(8,128)(2,1)} %copy-done.17, bf16[18,768]{1,0:T(8,128)(2,1)} %copy-done.16, ...), custom_call_target="tpu_custom_call" | custom-call | flops 8000000 | bytes 3000000 | tf_op jit(solution)/shard_map/tap_terms/pallas_call | solution.py:265
  66.4 1.2 fusion.16
  67.6 5.5 %collective-permute-done.11 = bf16[2,128,384]{2,1,0:T(8,128)(2,1)S(1)} collective-permute-done((bf16[2,128,384]{2,1,0:T(8,128)(2,1)S(1)}, bf16[2,128,384]{2,1,0:T(8,128)(2,1)S(1)}, u32[]{:S(2)}, u32[]{:S(2)}) %collective-permute-start.11) | collective-permute-done | bytes 196640 | tf_op jit(solution)/shard_map/ppermute | solution.py:433
  74.1 1.8 %collective-permute-start.12 = (bf16[4,128,384]{2,1,0:T(8,128)(2,1)S(1)}, bf16[4,128,384]{2,1,0:T(8,128)(2,1)}, u32[]{:S(2)}, u32[]{:S(2)}) collective-permute-start(bf16[4,128,384]{2,1,0:T(8,128)(2,1)S(1)} %pad_maximum_fusion.1.near), channel_id=1, source_target_pairs={{0,64},{16,80},{32,96},{48,112},{64,0},{80,16},{96,32},{112,48},{1... | collective-permute-start | bytes 1179656 | tf_op jit(solution)/shard_map/ppermute | solution.py:433
  76.0 1.2 add_convert_fusion.1
  78.5 8.9 %all-to-all-start.2 = ((bf16[64,24,384]{2,1,0:T(8,128)(2,1)}), bf16[64,24,384]{2,1,0:T(8,128)(2,1)S(1)}, u32[]{:S(2)}, u32[]{:S(2)}) async-start(bf16[64,24,384]{2,1,0:T(8,128)(2,1)} %bitcast.21), calls=%async_computation.2 | async-start | bytes 2359296 | tf_op jit(solution)/shard_map/all_to_all | solution.py:454
  87.4 3.6 %at_cells.1 = (f32[8,768]{1,0:T(8,128)}, bf16[128,8,128]{2,1,0:T(8,128)(2,1)}) custom-call(bf16[16,2,8,768]{3,2,1,0:T(8,128)(2,1)} %all-to-all-done.1.terms, bf16[768,768]{1,0:T(8,128)(2,1)} %w_key.3, bf16[768,768]{1,0:T(8,128)(2,1)} %w_value.3, f32[8,768]{1,0:T(8,128)} %get-tuple-element.30.standard, f32[8,128]{1,0:T(8,128)} %get-tuple-element.31.inverse, ...), custom_call_target="tpu_custom_call" | custom-call | flops 30000000 | bytes 3500000 | tf_op jit(solution)/shard_map/at_cells/pallas_call | solution.py:321
  92.7 1.8 %collective-permute-start.6 = (bf16[32,768]{1,0:T(8,128)(2,1)S(1)}, bf16[32,768]{1,0:T(8,128)(2,1)S(1)}, u32[]{:S(2)}, u32[]{:S(2)}) collective-permute-start(bf16[32,768]{1,0:T(8,128)(2,1)S(1)} %get-tuple-element.44), channel_id=1, source_target_pairs={{0,16},{16,32},{32,48},{48,64},{64,80},{80,96},{96,112},{112,0},{1... | collective-permute-start | bytes 147464 | tf_op jit(solution)/shard_map/ppermute | solution.py:33
  95.8 4.5 %collective-permute-done.6.top = bf16[32,768]{1,0:T(8,128)(2,1)S(1)} collective-permute-done((bf16[32,768]{1,0:T(8,128)(2,1)S(1)}, bf16[32,768]{1,0:T(8,128)(2,1)S(1)}, u32[]{:S(2)}, u32[]{:S(2)}) %collective-permute-start.6) | collective-permute-done | bytes 49184 | tf_op jit(solution)/shard_map/ppermute | solution.py:33
  100.3 3.3 %collective-permute-done.7.bottom = bf16[32,768]{1,0:T(8,128)(2,1)S(1)} collective-permute-done((bf16[32,768]{1,0:T(8,128)(2,1)S(1)}, bf16[32,768]{1,0:T(8,128)(2,1)S(1)}, u32[]{:S(2)}, u32[]{:S(2)}) %collective-permute-start.7) | collective-permute-done | bytes 49184 | tf_op jit(solution)/shard_map/ppermute | solution.py:34
  103.8 8.2 %all-to-all-start.3 = ((bf16[128,8,128]{2,1,0:T(8,128)(2,1)}), bf16[128,8,128]{2,1,0:T(8,128)(2,1)S(1)}, u32[]{:S(2)}, u32[]{:S(2)}) async-start(bf16[128,8,128]{2,1,0:T(8,128)(2,1)} %get-tuple-element.38), calls=%async_computation.3 | async-start | bytes 524288 | tf_op jit(solution)/shard_map/all_to_all | solution.py:464
  112.0 8.6 %all-to-all-done.3.blocks = bf16[128,8,128]{2,1,0:T(8,128)(2,1)S(1)} async-done(((bf16[128,8,128]{2,1,0:T(8,128)(2,1)}), bf16[128,8,128]{2,1,0:T(8,128)(2,1)S(1)}, u32[]{:S(2)}, u32[]{:S(2)}) %all-to-all-start.3) | async-done | bytes 262176 | tf_op jit(solution)/shard_map/all_to_all | solution.py:464
  121.3 2.7 %pieces.1 = (bf16[16,24,384]{2,1,0:T(8,128)(2,1)}, f32[8,128]{1,0:T(8,128)}) custom-call(s32[6]{0:T(128)} %pad_add_fusion.flags, bf16[64,24,384]{2,1,0:T(8,128)(2,1)} %copy-done.1, bf16[128,8,128]{2,1,0:T(8,128)(2,1)} %copy-done.5, bf16[4,128,384]{2,1,0:T(8,128)(2,1)} %copy-done.4, bf16[4,128,384]{2,1,0:T(8,128)(2,1)} %collective-permute-done.12.far), custom_call_target="tpu_custom_call" | custom-call | flops 100000000 | bytes 2500000 | tf_op jit(solution)/shard_map/pieces/pallas_call | solution.py:352
  124.0 4.6 %all-to-all-start.4 = ((bf16[16,24,384]{2,1,0:T(8,128)(2,1)}), bf16[16,24,384]{2,1,0:T(8,128)(2,1)S(1)}, u32[]{:S(2)}, u32[]{:S(2)}) async-start(bf16[16,24,384]{2,1,0:T(8,128)(2,1)} %get-tuple-element.39), calls=%async_computation.4 | async-start | bytes 589824 | tf_op jit(solution)/shard_map/all_to_all | solution.py:482
  128.6 4.7 %collective-permute-start.9 = (bf16[18,768]{1,0:T(8,128)(2,1)S(1)}, bf16[18,768]{1,0:T(8,128)(2,1)S(1)}, u32[]{:S(2)}, u32[]{:S(2)}) collective-permute-start(bf16[18,768]{1,0:T(8,128)(2,1)S(1)} %pad_maximum_fusion.6), channel_id=1, source_target_pairs={{1,0},{2,1},{3,2},{4,3},{5,4},{6,5},{7,6},{8,7},{9,8},{10,9},{11,1... | collective-permute-start | bytes 82952 | tf_op jit(solution)/shard_map/ppermute | solution.py:34
  133.4 1.8 %collective-permute-done.9.right = bf16[18,768]{1,0:T(8,128)(2,1)S(1)} collective-permute-done((bf16[18,768]{1,0:T(8,128)(2,1)S(1)}, bf16[18,768]{1,0:T(8,128)(2,1)S(1)}, u32[]{:S(2)}, u32[]{:S(2)}) %collective-permute-start.9) | collective-permute-done | bytes 27680 | tf_op jit(solution)/shard_map/ppermute | solution.py:34
  135.2 5.2 %collective-permute-done.8.left = bf16[18,768]{1,0:T(8,128)(2,1)S(1)} collective-permute-done((bf16[18,768]{1,0:T(8,128)(2,1)S(1)}, bf16[18,768]{1,0:T(8,128)(2,1)S(1)}, u32[]{:S(2)}, u32[]{:S(2)}) %collective-permute-start.8) | collective-permute-done | bytes 27680 | tf_op jit(solution)/shard_map/ppermute | solution.py:33
  141.0 4.3 %unmix.1 = bf16[16,32,768]{2,1,0:T(8,128)(2,1)} custom-call(s32[6]{0:T(128)} %pad_add_fusion.flags, f32[16,32,768]{2,1,0:T(8,128)} %bitcast.66, f32[8,768]{1,0:T(8,128)} %get-tuple-element.34.pooled, bf16[32,768]{1,0:T(8,128)(2,1)} %copy-done.14, bf16[32,768]{1,0:T(8,128)(2,1)} %copy-done.15, bf16[18,768]{1,0:T(8,128)(2,1)} %copy-done.19, ...), custom_call_target="tpu_custom_call" | custom-call | flops 8000000 | bytes 3000000 | tf_op jit(solution)/shard_map/unmix/pallas_call | solution.py:389
  (96 shorter events, 16.8 us)
Async XLA Ops:
  0.6 28.1 %copy-start = (bf16[768,768]{1,0:T(8,128)(2,1)S(1)}, bf16[768,768]{1,0:T(8,128)(2,1)}, u32[]{:S(2)}) copy-start(bf16[768,768]{1,0:T(8,128)(2,1)} %param.9) | copy-start | bytes 3538948
  1.6 6.6 %collective-permute-start = (bf16[32,768]{1,0:T(8,128)(2,1)S(1)}, bf16[32,768]{1,0:T(8,128)(2,1)S(1)}, u32[]{:S(2)}, u32[]{:S(2)}) collective-permute-start(bf16[32,768]{1,0:T(8,128)(2,1)S(1)} %get-tuple-element.48), channel_id=1, source_target_pairs={{0,16},{16,32},{32,48},{48,64},{64,80},{80,96},{96,112},{112,0},{1... | collective-permute-start | bytes 147464 | tf_op jit(solution)/shard_map/ppermute | solution.py:33
  3.0 5.3 %collective-permute-start.1 = (bf16[32,768]{1,0:T(8,128)(2,1)S(1)}, bf16[32,768]{1,0:T(8,128)(2,1)S(1)}, u32[]{:S(2)}, u32[]{:S(2)}) collective-permute-start(bf16[32,768]{1,0:T(8,128)(2,1)S(1)} %get-tuple-element.47), channel_id=1, source_target_pairs={{16,0},{32,16},{48,32},{64,48},{80,64},{96,80},{112,96},{0,112},{1... | collective-permute-start | bytes 147464 | tf_op jit(solution)/shard_map/ppermute | solution.py:34
  8.2 9.2 %copy-start.9 = (bf16[32,768]{1,0:T(8,128)(2,1)}, bf16[32,768]{1,0:T(8,128)(2,1)S(1)}, u32[]{:S(2)}) copy-start(bf16[32,768]{1,0:T(8,128)(2,1)S(1)} %collective-permute-done.top) | copy-start | bytes 147460
  8.2 9.1 %copy-start.10 = (bf16[32,768]{1,0:T(8,128)(2,1)}, bf16[32,768]{1,0:T(8,128)(2,1)S(1)}, u32[]{:S(2)}) copy-start(bf16[32,768]{1,0:T(8,128)(2,1)S(1)} %collective-permute-done.1.bottom) | copy-start | bytes 147460
  8.3 3.6 %collective-permute-start.3 = (bf16[18,768]{1,0:T(8,128)(2,1)S(1)}, bf16[18,768]{1,0:T(8,128)(2,1)S(1)}, u32[]{:S(2)}, u32[]{:S(2)}) collective-permute-start(bf16[18,768]{1,0:T(8,128)(2,1)S(1)} %pad_maximum_fusion.4), channel_id=1, source_target_pairs={{1,0},{2,1},{3,2},{4,3},{5,4},{6,5},{7,6},{8,7},{9,8},{10,9},{11,1... | collective-permute-start | bytes 82952 | tf_op jit(solution)/shard_map/ppermute | solution.py:34
  10.3 7.1 %collective-permute-start.2 = (bf16[18,768]{1,0:T(8,128)(2,1)S(1)}, bf16[18,768]{1,0:T(8,128)(2,1)S(1)}, u32[]{:S(2)}, u32[]{:S(2)}) collective-permute-start(bf16[18,768]{1,0:T(8,128)(2,1)S(1)} %pad_maximum_fusion.3), channel_id=1, source_target_pairs={{0,1},{1,2},{2,3},{3,4},{4,5},{5,6},{6,7},{7,8},{8,9},{9,10},{10,1... | collective-permute-start | bytes 82952 | tf_op jit(solution)/shard_map/ppermute | solution.py:33
  11.9 5.5 %copy-start.16 = (bf16[18,768]{1,0:T(8,128)(2,1)}, bf16[18,768]{1,0:T(8,128)(2,1)S(1)}, u32[]{:S(2)}) copy-start(bf16[18,768]{1,0:T(8,128)(2,1)S(1)} %collective-permute-done.3.right) | copy-start | bytes 82948
  22.4 12.0 %all-to-all-start = ((bf16[16,8,768]{2,1,0:T(8,128)(2,1)}), bf16[16,8,768]{2,1,0:T(8,128)(2,1)S(1)}, u32[]{:S(2)}, u32[]{:S(2)}) async-start(bf16[16,8,768]{2,1,0:T(8,128)(2,1)} %get-tuple-element.23), calls=%async_computation | async-start | bytes 393216 | tf_op jit(solution)/shard_map/all_to_all | solution.py:428
  35.1 8.0 %copy-start.2 = (bf16[16,32,768]{2,1,0:T(8,128)(2,1)S(1)}, bf16[16,32,768]{2,1,0:T(8,128)(2,1)}, u32[]{:S(2)}) copy-start(bf16[16,32,768]{2,1,0:T(8,128)(2,1)} %param.13) | copy-start | bytes 2359300
  43.1 3.3 %copy-start.3 = (bf16[768,512]{1,0:T(8,128)(2,1)S(1)}, bf16[768,512]{1,0:T(8,128)(2,1)}, u32[]{:S(2)}) copy-start(bf16[768,512]{1,0:T(8,128)(2,1)} %get-tuple-element.24) | copy-start | bytes 2359300
  43.1 3.3 %copy-start.7 = (bf16[512,768]{1,0:T(8,128)(2,1)S(1)}, bf16[512,768]{1,0:T(8,128)(2,1)}, u32[]{:S(2)}) copy-start(bf16[512,768]{1,0:T(8,128)(2,1)} %get-tuple-element.22) | copy-start | bytes 2359300
  47.3 18.7 %copy-start.6 = (bf16[1,128,384]{2,1,0:T(8,128)(2,1)}, bf16[1,128,384]{2,1,0:T(8,128)(2,1)S(1)}, u32[]{:S(2)}) copy-start(bf16[1,128,384]{2,1,0:T(8,128)(2,1)S(1)} %dynamic-slice_bitcast_fusion) | copy-start | bytes 294916
  49.7 26.3 %collective-permute-start.4 = (bf16[768,384]{1,0:T(8,128)(2,1)}, bf16[768,384]{1,0:T(8,128)(2,1)}, u32[]{:S(2)}, u32[]{:S(2)}) collective-permute-start(bf16[768,384]{1,0:T(8,128)(2,1)} %convolution_convert_fusion.3), channel_id=1, source_target_pairs={{0,1},{1,0},{2,3},{3,2},{4,5},{5,4},{6,7},{7,6},{8,9},{9,8},{10,11... | collective-permute-start | bytes 1769480 | tf_op jit(solution)/shard_map/ppermute | solution.py:448
  50.0 16.1 %collective-permute-start.10 = (bf16[1,128,384]{2,1,0:T(8,128)(2,1)S(1)}, bf16[1,128,384]{2,1,0:T(8,128)(2,1)S(1)}, u32[]{:S(2)}, u32[]{:S(2)}) collective-permute-start(bf16[1,128,384]{2,1,0:T(8,128)(2,1)S(1)} %dynamic-slice_bitcast_fusion), channel_id=1, source_target_pairs={{0,16},{16,0},{32,48},{48,32},{64,80},{80,64},{96,112},{112,96},{1... | collective-permute-start | bytes 294920 | tf_op jit(solution)/shard_map/ppermute | solution.py:433
  53.9 23.2 %collective-permute-start.5 = (bf16[768,384]{1,0:T(8,128)(2,1)}, bf16[768,384]{1,0:T(8,128)(2,1)S(1)}, u32[]{:S(2)}, u32[]{:S(2)}) collective-permute-start(bf16[768,384]{1,0:T(8,128)(2,1)} %fusion.1), channel_id=1, source_target_pairs={{0,1},{1,0},{2,3},{3,2},{4,5},{5,4},{6,7},{7,6},{8,9},{9,8},{10,11... | collective-permute-start | bytes 1769480 | tf_op jit(solution)/shard_map/ppermute | solution.py:448
  53.9 24.6 %all-to-all-start.1 = ((bf16[16,2,8,768]{3,2,1,0:T(8,128)(2,1)}), bf16[16,2,8,768]{3,2,1,0:T(8,128)(2,1)}, u32[]{:S(2)}, u32[]{:S(2)}) async-start(bf16[16,2,8,768]{3,2,1,0:T(8,128)(2,1)} %get-tuple-element.28), calls=%async_computation.1 | async-start | bytes 786432 | tf_op jit(solution)/shard_map/all_to_all | solution.py:437
  66.1 7.0 %collective-permute-start.11 = (bf16[2,128,384]{2,1,0:T(8,128)(2,1)S(1)}, bf16[2,128,384]{2,1,0:T(8,128)(2,1)S(1)}, u32[]{:S(2)}, u32[]{:S(2)}) collective-permute-start(bf16[2,128,384]{2,1,0:T(8,128)(2,1)S(1)} %pad_maximum_fusion.2), channel_id=1, source_target_pairs={{0,32},{16,48},{32,0},{48,16},{64,96},{80,112},{96,64},{112,80},{1... | collective-permute-start | bytes 589832 | tf_op jit(solution)/shard_map/ppermute | solution.py:433
  74.1 3.2 %copy-start.4 = (bf16[4,128,384]{2,1,0:T(8,128)(2,1)}, bf16[4,128,384]{2,1,0:T(8,128)(2,1)S(1)}, u32[]{:S(2)}) copy-start(bf16[4,128,384]{2,1,0:T(8,128)(2,1)S(1)} %pad_maximum_fusion.1.near) | copy-start | bytes 1179652
  74.1 37.9 %collective-permute-start.12 = (bf16[4,128,384]{2,1,0:T(8,128)(2,1)S(1)}, bf16[4,128,384]{2,1,0:T(8,128)(2,1)}, u32[]{:S(2)}, u32[]{:S(2)}) collective-permute-start(bf16[4,128,384]{2,1,0:T(8,128)(2,1)S(1)} %pad_maximum_fusion.1.near), channel_id=1, source_target_pairs={{0,64},{16,80},{32,96},{48,112},{64,0},{80,16},{96,32},{112,48},{1... | collective-permute-start | bytes 1179656 | tf_op jit(solution)/shard_map/ppermute | solution.py:433
  78.5 25.3 %all-to-all-start.2 = ((bf16[64,24,384]{2,1,0:T(8,128)(2,1)}), bf16[64,24,384]{2,1,0:T(8,128)(2,1)S(1)}, u32[]{:S(2)}, u32[]{:S(2)}) async-start(bf16[64,24,384]{2,1,0:T(8,128)(2,1)} %bitcast.21), calls=%async_computation.2 | async-start | bytes 2359296 | tf_op jit(solution)/shard_map/all_to_all | solution.py:454
  92.7 7.5 %collective-permute-start.6 = (bf16[32,768]{1,0:T(8,128)(2,1)S(1)}, bf16[32,768]{1,0:T(8,128)(2,1)S(1)}, u32[]{:S(2)}, u32[]{:S(2)}) collective-permute-start(bf16[32,768]{1,0:T(8,128)(2,1)S(1)} %get-tuple-element.44), channel_id=1, source_target_pairs={{0,16},{16,32},{32,48},{48,64},{64,80},{80,96},{96,112},{112,0},{1... | collective-permute-start | bytes 147464 | tf_op jit(solution)/shard_map/ppermute | solution.py:33
  94.6 9.1 %collective-permute-start.7 = (bf16[32,768]{1,0:T(8,128)(2,1)S(1)}, bf16[32,768]{1,0:T(8,128)(2,1)S(1)}, u32[]{:S(2)}, u32[]{:S(2)}) collective-permute-start(bf16[32,768]{1,0:T(8,128)(2,1)S(1)} %get-tuple-element.43), channel_id=1, source_target_pairs={{16,0},{32,16},{48,32},{64,48},{80,64},{96,80},{112,96},{0,112},{1... | collective-permute-start | bytes 147464 | tf_op jit(solution)/shard_map/ppermute | solution.py:34
  100.3 23.7 %copy-start.14 = (bf16[32,768]{1,0:T(8,128)(2,1)}, bf16[32,768]{1,0:T(8,128)(2,1)S(1)}, u32[]{:S(2)}) copy-start(bf16[32,768]{1,0:T(8,128)(2,1)S(1)} %collective-permute-done.6.top) | copy-start | bytes 147460
  103.6 20.4 %copy-start.15 = (bf16[32,768]{1,0:T(8,128)(2,1)}, bf16[32,768]{1,0:T(8,128)(2,1)S(1)}, u32[]{:S(2)}) copy-start(bf16[32,768]{1,0:T(8,128)(2,1)S(1)} %collective-permute-done.7.bottom) | copy-start | bytes 147460
  103.8 16.8 %copy-start.1 = (bf16[64,24,384]{2,1,0:T(8,128)(2,1)}, bf16[64,24,384]{2,1,0:T(8,128)(2,1)S(1)}, u32[]{:S(2)}) copy-start(bf16[64,24,384]{2,1,0:T(8,128)(2,1)S(1)} %all-to-all-done.2.got) | copy-start | bytes 3538948
  103.8 16.8 %all-to-all-start.3 = ((bf16[128,8,128]{2,1,0:T(8,128)(2,1)}), bf16[128,8,128]{2,1,0:T(8,128)(2,1)S(1)}, u32[]{:S(2)}, u32[]{:S(2)}) async-start(bf16[128,8,128]{2,1,0:T(8,128)(2,1)} %get-tuple-element.38), calls=%async_computation.3 | async-start | bytes 524288 | tf_op jit(solution)/shard_map/all_to_all | solution.py:464
  124.0 22.0 %all-to-all-start.4 = ((bf16[16,24,384]{2,1,0:T(8,128)(2,1)}), bf16[16,24,384]{2,1,0:T(8,128)(2,1)S(1)}, u32[]{:S(2)}, u32[]{:S(2)}) async-start(bf16[16,24,384]{2,1,0:T(8,128)(2,1)} %get-tuple-element.39), calls=%async_computation.4 | async-start | bytes 589824 | tf_op jit(solution)/shard_map/all_to_all | solution.py:482
  128.6 6.6 %collective-permute-start.9 = (bf16[18,768]{1,0:T(8,128)(2,1)S(1)}, bf16[18,768]{1,0:T(8,128)(2,1)S(1)}, u32[]{:S(2)}, u32[]{:S(2)}) collective-permute-start(bf16[18,768]{1,0:T(8,128)(2,1)S(1)} %pad_maximum_fusion.6), channel_id=1, source_target_pairs={{1,0},{2,1},{3,2},{4,3},{5,4},{6,5},{7,6},{8,7},{9,8},{10,9},{11,1... | collective-permute-start | bytes 82952 | tf_op jit(solution)/shard_map/ppermute | solution.py:34
  133.3 12.0 %copy-start.20 = (f32[8,128]{1,0:T(8,128)S(1)}, f32[8,128]{1,0:T(8,128)}, u32[]{:S(2)}) copy-start(f32[8,128]{1,0:T(8,128)} %get-tuple-element.40) | copy-start | bytes 12292
  133.3 7.1 %collective-permute-start.8 = (bf16[18,768]{1,0:T(8,128)(2,1)S(1)}, bf16[18,768]{1,0:T(8,128)(2,1)S(1)}, u32[]{:S(2)}, u32[]{:S(2)}) collective-permute-start(bf16[18,768]{1,0:T(8,128)(2,1)S(1)} %pad_maximum_fusion.5), channel_id=1, source_target_pairs={{0,1},{1,2},{2,3},{3,4},{4,5},{5,6},{6,7},{7,8},{8,9},{9,10},{10,1... | collective-permute-start | bytes 82952 | tf_op jit(solution)/shard_map/ppermute | solution.py:33
  135.2 5.2 %copy-start.18 = (bf16[18,768]{1,0:T(8,128)(2,1)}, bf16[18,768]{1,0:T(8,128)(2,1)S(1)}, u32[]{:S(2)}) copy-start(bf16[18,768]{1,0:T(8,128)(2,1)S(1)} %collective-permute-done.9.right) | copy-start | bytes 82948
  (7 other events, 6.3 us)
where the time goes:
time: 149 us; the launch traced here: 147 us
  starting transfers between devices  51.4 us (34%)
  waiting for transfers between devices  38.3 us (26%)
  Pallas kernels  27.6 us (19%)
  matrix products  13.3 us (9%)
  local copies, waits for them, and re-layouts  9.36 us (6%)
  other arithmetic  5.89 us (4%)
    ppermute x4, waiting for transfers between devices, from_both_sides(): lax.ppermute(last, axis, [(i, (i + 1) % count) for i in range(count)])  15.1 us
    dot_general x6, matrix products, dot(): lax.dot_general(left, right, ((dims[0], dims[1]), ((), ())), preferred_el...  10.5 us
    all_to_all x1, starting transfers between devices, block_gradients(): lax.all_to_all(chip.reshape(64, 24, half), BOTH, 0, 0, tiled=True, axis_i...  8.87 us
    all_to_all x1, waiting for transfers between devices, block_gradients(): blocks = lax.all_to_all(block, BOTH, 0, 0, tiled=True)  8.6 us
    all_to_all x1, starting transfers between devices, block_gradients(): blocks = lax.all_to_all(block, BOTH, 0, 0, tiled=True)  8.15 us
    pallas_call x1, Pallas kernels, attend(): pl.pallas_call(attend_kernel, grid=(channels // LANES,), in_specs=[by_pai...  8.01 us
    all_to_all x1, starting transfers between devices, block_gradients(): terms = lax.all_to_all(sums, 'col', 0, 0, tiled=True)  7.57 us
    ppermute x4, starting transfers between devices, from_both_sides(): lax.ppermute(first, axis, [((i + 1) % count, i) for i in range(count)])  7.56 us
  transfers between devices with their start and end apart: 18, of which 10 were waited for; matrix products, arithmetic and copies ran while one was open for 12% of the time, Pallas kernels for 8%

commit v1 on v0

--- a/solution.py
+++ b/solution.py
@@ -17,6 +17,7 @@
 PARTNER = (5, 4, 7, 6, 9, 8, 11, 10)
 SLICE_AT = tuple((FINAL.index(j) if j in FINAL else PARTNER.index(j)) for j in range(16))
 PAIRS = [(j, j ^ 1) for j in range(16)]
+OTHER_PAIRS = [(j, (j + (1 if j % 2 else -1)) % 16) for j in range(16)]
 BOTH = ("row", "col")
 
 
@@ -33,6 +34,13 @@
     before = lax.ppermute(last, axis, [(i, (i + 1) % count) for i in range(count)])
     after = lax.ppermute(first, axis, [((i + 1) % count, i) for i in range(count)])
     return before, after
+
+
+def column_sides(first, last):
+    odd = lax.axis_index("col") % 2 == 1
+    near = lax.ppermute(jnp.where(odd, first, last), "col", PAIRS)
+    far = lax.ppermute(jnp.where(odd, last, first), "col", OTHER_PAIRS)
+    return jnp.where(odd, near, far), jnp.where(odd, far, near)
 
 
 def edges_of(tile, is_first, is_last):
@@ -41,7 +49,7 @@
     down = jnp.where(is_last, 0, bottom).astype(BF)
     first = jnp.concatenate([up[:1], tile[:, 0], down[:1]], axis=0)
     last = jnp.concatenate([up[-1:], tile[:, -1], down[-1:]], axis=0)
-    left, right = from_both_sides(first, last, "col")
+    left, right = column_sides(first, last)
     return top, bottom, left, right
 
 
@@ -161,6 +169,7 @@
             pltpu.VMEM((18, 48, WIDE), F32),
             pltpu.VMEM((channels // LANES, 8, LANES), F32),
         ],
+        compiler_params=pltpu.CompilerParams(vmem_limit_bytes=16 << 20),
         cost_estimate=pl.CostEstimate(flops=8_000_000, bytes_accessed=2_000_000, transcendentals=0),
         name="mix",
     )(flags, image, *sides, taps)
@@ -226,6 +235,26 @@
         ),
         name="attend",
     )(query, dout, cells, w_key, w_value)
+
+
+def chip_kernel(own_query, their_query, own_out, their_out, chip):
+    chip[0] = (own_query[...].astype(F32) + their_query[...].astype(F32)).astype(BF)
+    chip[1] = (own_out[...].astype(F32) + their_out[...].astype(F32)).astype(BF)
+
+
+def chip_sums(own, theirs):
+    rows, half = own[0].shape
+    block = pl.BlockSpec((rows // 2, half), lambda i: (i, 0))
+    return pl.pallas_call(
+        chip_kernel,
+        grid=(2,),
+        in_specs=[block] * 4,
+        out_specs=pl.BlockSpec((2, rows // 2, half), lambda i: (0, i, 0)),
+        out_shape=jax.ShapeDtypeStruct((2, rows, half), BF),
+        compiler_params=pltpu.CompilerParams(vmem_limit_bytes=16 << 20),
+        cost_estimate=pl.CostEstimate(flops=1_200_000, bytes_accessed=3_500_000, transcendentals=0),
+        name="chip_sums",
+    )(own[0], theirs[0], own[1], theirs[1])
 
 
 def taps_kernel(flags, image, top, bottom, left, right, early, terms, windows, padded, lines):
@@ -275,6 +304,7 @@
             jax.ShapeDtypeStruct((9, 8, channels), F32),
         ],
         scratch_shapes=[pltpu.VMEM((18, 48, WIDE), F32), pltpu.VMEM((48, WIDE), F32)],
+        compiler_params=pltpu.CompilerParams(vmem_limit_bytes=16 << 20),
         cost_estimate=pl.CostEstimate(flops=8_000_000, bytes_accessed=3_000_000, transcendentals=0),
         name="tap_terms",
     )(flags, image, *sides, early)
@@ -324,6 +354,7 @@
             jax.ShapeDtypeStruct((8, channels), F32),
             jax.ShapeDtypeStruct((128, 8, LANES), BF),
         ],
+        compiler_params=pltpu.CompilerParams(vmem_limit_bytes=16 << 20),
         cost_estimate=pl.CostEstimate(flops=30_000_000, bytes_accessed=3_500_000, transcendentals=0),
         name="at_cells",
     )(terms, w_key, w_value, standard, inverse, early, windows)
@@ -356,6 +387,7 @@
             jax.ShapeDtypeStruct((16, 24, half), BF),
             jax.ShapeDtypeStruct((8, LANES), F32),
         ],
+        compiler_params=pltpu.CompilerParams(vmem_limit_bytes=16 << 20),
         cost_estimate=pl.CostEstimate(flops=100_000_000, bytes_accessed=2_500_000, transcendentals=0),
         name="pieces",
     )(flags, got, blocks, near, far)
@@ -399,6 +431,7 @@
         out_specs=block,
         out_shape=jax.ShapeDtypeStruct((height, width, channels), BF),
         scratch_shapes=[pltpu.VMEM((18, 48, WIDE), F32)],
+        compiler_params=pltpu.CompilerParams(vmem_limit_bytes=16 << 20),
         cost_estimate=pl.CostEstimate(flops=8_000_000, bytes_accessed=3_000_000, transcendentals=0),
         name="unmix",
     )(flags, early, pooled, *sides, taps)
@@ -447,9 +480,7 @@
     sent = half_terms(1 - core)
     theirs = [lax.ppermute(x, "col", PAIRS) for x in sent]
     own = lax.optimization_barrier(half_terms(core))
-    chip = jnp.concatenate(
-        [x.astype(F32) + y.astype(F32) for x, y in zip(own, theirs)], axis=0
-    ).astype(BF)
+    chip = chip_sums(own, theirs)
     chip, terms = lax.optimization_barrier((chip, terms))
     got = lax.all_to_all(
         chip.reshape(64, 24, half), BOTH, 0, 0, tiled=True, axis_index_groups=SUM_GROUPS
@@ -472,10 +503,9 @@
     last = (early[:, -1] + jnp.repeat(down, POOL, axis=0)).astype(BF)
     over = jnp.where(is_first, 0, top).astype(BF)
     under = jnp.where(is_last, 0, bottom).astype(BF)
-    left, right = from_both_sides(
+    left, right = column_sides(
         jnp.concatenate([over[:1], first, under[:1]], axis=0),
         jnp.concatenate([over[-1:], last, under[-1:]], axis=0),
-        "col",
     )
     grad_image = unmix(flags, early, pooled, (top, bottom, left, right), conv_taps)
     placed, conv = pieces(flags, got, blocks, near, far)

time: 149 us -> 155 us (1.040)
  the two profiles are of different devices: /device:TPU:96 before, /device:TPU:1 now
where the time goes in v1:
time: 155 us; the launch traced here: 154 us
  starting transfers between devices  54.8 us (35%)
  waiting for transfers between devices  36 us (23%)
  Pallas kernels  23.2 us (15%)
  local copies, waits for them, and re-layouts  20.5 us (13%)
  matrix products  13 us (8%)
  other arithmetic  5.02 us (3%)
    unnamed x76, local copies, waits for them, and re-layouts  15.3 us
    ppermute x2, waiting for transfers between devices, from_both_sides(): lax.ppermute(last, axis, [(i, (i + 1) % count) for i in range(count)])  12.6 us
    dot_general x6, matrix products, dot(): lax.dot_general(left, right, ((dims[0], dims[1]), ((), ())), preferred_el...  11.3 us
    all_to_all x1, starting transfers between devices, block_gradients(): cells = lax.all_to_all(normed, 'col', 0, 0, tiled=True)  11.3 us
    all_to_all x1, starting transfers between devices, block_gradients(): lax.all_to_all(chip.reshape(64, 24, half), BOTH, 0, 0, tiled=True, axis_i...  10.5 us
    all_to_all x1, starting transfers between devices, block_gradients(): blocks = lax.all_to_all(block, BOTH, 0, 0, tiled=True)  8.16 us
    all_to_all x1, waiting for transfers between devices, block_gradients(): blocks = lax.all_to_all(block, BOTH, 0, 0, tiled=True)  8.16 us
    pallas_call x1, Pallas kernels, attend(): pl.pallas_call(attend_kernel, grid=(channels // LANES,), in_specs=[by_pai...  7.92 us
  transfers between devices with their start and end apart: 18, of which 6 were waited for; matrix products, arithmetic and copies ran while one was open for 10% of the time, Pallas kernels for 8%

profile of v1, /device:TPU:1, one launch (start us, length us, event | category | flops | bytes accessed | tf_op | source)
XLA Modules:
  0.0 153.6 jit_solution(5204632287930066925)
XLA Ops:
  1.6 2.5 %collective-permute-start = (bf16[32,768]{1,0:T(8,128)(2,1)S(1)}, bf16[32,768]{1,0:T(8,128)(2,1)S(1)}, u32[]{:S(2)}, u32[]{:S(2)}) collective-permute-start(bf16[32,768]{1,0:T(8,128)(2,1)S(1)} %get-tuple-element.48), channel_id=1, source_target_pairs={{0,16},{16,32},{32,48},{48,64},{64,80},{80,96},{96,112},{112,0},{1... | collective-permute-start | bytes 147464 | tf_op jit(solution)/shard_map/ppermute | solution.py:34
  4.1 2.3 %collective-permute-start.1 = (bf16[32,768]{1,0:T(8,128)(2,1)S(1)}, bf16[32,768]{1,0:T(8,128)(2,1)S(1)}, u32[]{:S(2)}, u32[]{:S(2)}) collective-permute-start(bf16[32,768]{1,0:T(8,128)(2,1)S(1)} %get-tuple-element.47), channel_id=1, source_target_pairs={{16,0},{32,16},{48,32},{64,48},{80,64},{96,80},{112,96},{0,112},{1... | collective-permute-start | bytes 147464 | tf_op jit(solution)/shard_map/ppermute | solution.py:35
  7.5 3.3 %convolution_convert_fusion.dout = bf16[512,768]{1,0:T(8,128)(2,1)} fusion(bf16[512,768]{1,0:T(8,128)(2,1)} %bitcast.66, bf16[768,768]{1,0:T(8,128)(2,1)} %param.12), kind=kOutput, calls=%fused_computation.1 | convolution fusion | flops 604372992 | bytes 2752512 | tf_op jit(solution)/shard_map/dot_general | solution.py:57
  12.1 1.3 collective-permute-start.3
  13.5 2.0 %collective-permute-done.3 = bf16[18,768]{1,0:T(8,128)(2,1)S(1)} collective-permute-done((bf16[18,768]{1,0:T(8,128)(2,1)S(1)}, bf16[18,768]{1,0:T(8,128)(2,1)S(1)}, u32[]{:S(2)}, u32[]{:S(2)}) %collective-permute-start.3) | collective-permute-done | bytes 27680 | tf_op jit(solution)/shard_map/ppermute | solution.py:42
  15.6 3.7 %mix.1 = (bf16[512,768]{1,0:T(8,128)(2,1)S(1)}, f32[8,768]{1,0:T(8,128)S(1)}, f32[8,128]{1,0:T(8,128)S(1)}, bf16[16,8,768]{2,1,0:T(8,128)(2,1)}) custom-call(s32[6]{0:T(128)S(1)} %pad_add_fusion.flags, bf16[16,32,768]{2,1,0:T(8,128)(2,1)S(1)} %copy-done.2, bf16[32,768]{1,0:T(8,128)(2,1)S(1)} %collective-permute-done.top, ...), custom_call_target="tpu_custom_call" | custom-call | flops 8000000 | bytes 2000000 | tf_op jit(solution)/shard_map/mix/pallas_call | solution.py:147
  20.5 11.3 %all-to-all-start = ((bf16[16,8,768]{2,1,0:T(8,128)(2,1)}), bf16[16,8,768]{2,1,0:T(8,128)(2,1)S(1)}, u32[]{:S(2)}, u32[]{:S(2)}) async-start(bf16[16,8,768]{2,1,0:T(8,128)(2,1)} %get-tuple-element.23), calls=%async_computation | async-start | bytes 393216 | tf_op jit(solution)/shard_map/all_to_all | solution.py:461
  31.8 1.7 %convolution_convert_fusion.1.query = bf16[512,768]{1,0:T(8,128)(2,1)} fusion(bf16[512,768]{1,0:T(8,128)(2,1)S(1)} %get-tuple-element.22, bf16[768,768]{1,0:T(8,128)(2,1)S(1)} %copy-done), kind=kOutput, calls=%fused_computation.2 | convolution fusion | flops 604372992 | bytes 2752512 | tf_op jit(solution)/shard_map/dot_general | solution.py:463
  33.5 6.4 %all-to-all-done = bf16[16,8,768]{2,1,0:T(8,128)(2,1)S(1)} async-done(((bf16[16,8,768]{2,1,0:T(8,128)(2,1)}), bf16[16,8,768]{2,1,0:T(8,128)(2,1)S(1)}, u32[]{:S(2)}, u32[]{:S(2)}) %all-to-all-start) | async-done | bytes 196640 | tf_op jit(solution)/shard_map/all_to_all | solution.py:461
  40.6 7.9 %attend.1 = (bf16[768,512]{1,0:T(8,128)(2,1)}, bf16[768,512]{1,0:T(8,128)(2,1)}, bf16[16,2,8,768]{3,2,1,0:T(8,128)(2,1)}) custom-call(bf16[512,768]{1,0:T(8,128)(2,1)} %convolution_convert_fusion.1.query, bf16[512,768]{1,0:T(8,128)(2,1)} %convolution_convert_fusion.dout, bf16[128,768]{1,0:T(8,128)(2,1)} %bitcast.72, bf16[768,768]{1,0:T(8,128)(2,1)} %w_key.3, ...), custom_call_target="tpu_custom_call" | custom-call | flops 3000000000 | bytes 6000000 | tf_op jit(solution)/shard_map/attend/pallas_call | solution.py:217
  48.5 2.3 %convert_add_fusion = f32[512,768]{1,0:T(8,128)S(1)} fusion(bf16[512,768]{1,0:T(8,128)(2,1)} %bitcast.67, bf16[768,512]{1,0:T(8,128)(2,1)} %get-tuple-element.24, bf16[768,768]{1,0:T(8,128)(2,1)S(1)} %copy-done), kind=kOutput, calls=%fused_computation | convolution fusion | flops 604766208 | bytes 4325376 | tf_op jit(solution)/shard_map/dot_general | solution.py:57
  50.9 1.4 convolution_convert_fusion.5.own_query
  52.9 1.4 convolution_convert_fusion.3
  54.9 1.5 fusion.1
  56.3 1.4 fusion.own_out
  57.8 4.5 %all-to-all-start.1 = ((bf16[16,2,8,768]{3,2,1,0:T(8,128)(2,1)}), bf16[16,2,8,768]{3,2,1,0:T(8,128)(2,1)}, u32[]{:S(2)}, u32[]{:S(2)}) async-start(bf16[16,2,8,768]{3,2,1,0:T(8,128)(2,1)} %get-tuple-element.28), calls=%async_computation.1 | async-start | bytes 786432 | tf_op jit(solution)/shard_map/all_to_all | solution.py:470
  65.4 2.9 %tap_terms.1 = (f32[9,768]{1,0:T(8,128)S(1)}, f32[9,8,768]{2,1,0:T(8,128)S(1)}) custom-call(s32[6]{0:T(128)S(1)} %pad_add_fusion.flags, bf16[16,32,768]{2,1,0:T(8,128)(2,1)S(1)} %copy-done.2, bf16[32,768]{1,0:T(8,128)(2,1)S(1)} %copy-done.10, bf16[32,768]{1,0:T(8,128)(2,1)S(1)} %copy-done.12, bf16[18,768]{1,0:T(8,128)(2,1)S(1)} %copy-done.16, ...), custom_call_target="tpu_custom_call" | custom-call | flops 8000000 | bytes 3000000 | tf_op jit(solution)/shard_map/tap_terms/pallas_call | solution.py:294
  71.6 5.4 %collective-permute-done.11 = bf16[2,128,384]{2,1,0:T(8,128)(2,1)S(1)} collective-permute-done((bf16[2,128,384]{2,1,0:T(8,128)(2,1)S(1)}, bf16[2,128,384]{2,1,0:T(8,128)(2,1)S(1)}, u32[]{:S(2)}, u32[]{:S(2)}) %collective-permute-start.11) | collective-permute-done | bytes 196640 | tf_op jit(solution)/shard_map/ppermute | solution.py:466
  77.9 1.7 %collective-permute-start.12 = (bf16[4,128,384]{2,1,0:T(8,128)(2,1)S(1)}, bf16[4,128,384]{2,1,0:T(8,128)(2,1)}, u32[]{:S(2)}, u32[]{:S(2)}) collective-permute-start(bf16[4,128,384]{2,1,0:T(8,128)(2,1)S(1)} %pad_maximum_fusion.near), channel_id=1, source_target_pairs={{0,64},{16,80},{32,96},{48,112},{64,0},{80,16},{96,32},{112,48},{1... | collective-permute-start | bytes 1179656 | tf_op jit(solution)/shard_map/ppermute | solution.py:466
  79.7 1.5 chip_sums.1
  82.2 1.3 copy-done.5
  83.5 1.3 copy-done.6
  87.2 2.1 %at_cells.1 = (f32[8,768]{1,0:T(8,128)S(1)}, bf16[128,8,128]{2,1,0:T(8,128)(2,1)S(1)}) custom-call(bf16[16,2,8,768]{3,2,1,0:T(8,128)(2,1)} %all-to-all-done.1.terms, bf16[768,768]{1,0:T(8,128)(2,1)S(1)} %copy-done.5, bf16[768,768]{1,0:T(8,128)(2,1)S(1)} %copy-done.6, f32[8,768]{1,0:T(8,128)S(1)} %copy-done.30, f32[8,128]{1,0:T(8,128)S(1)} %get-tuple-element.31.inverse, ...), custom_call_target="tpu_custom_call" | custom-call | flops 30000000 | bytes 3500000 | tf_op jit(solution)/shard_map/at_cells/pallas_call | solution.py:351
  90.6 10.5 %all-to-all-start.2 = ((bf16[64,24,384]{2,1,0:T(8,128)(2,1)}), bf16[64,24,384]{2,1,0:T(8,128)(2,1)}, u32[]{:S(2)}, u32[]{:S(2)}) async-start(bf16[64,24,384]{2,1,0:T(8,128)(2,1)} %bitcast.65), calls=%async_computation.2 | async-start | bytes 2359296 | tf_op jit(solution)/shard_map/all_to_all | solution.py:485
  102.4 2.4 %collective-permute-start.7 = (bf16[32,768]{1,0:T(8,128)(2,1)S(1)}, bf16[32,768]{1,0:T(8,128)(2,1)S(1)}, u32[]{:S(2)}, u32[]{:S(2)}) collective-permute-start(bf16[32,768]{1,0:T(8,128)(2,1)S(1)} %get-tuple-element.43), channel_id=1, source_target_pairs={{16,0},{32,16},{48,32},{64,48},{80,64},{96,80},{112,96},{0,112},{1... | collective-permute-start | bytes 147464 | tf_op jit(solution)/shard_map/ppermute | solution.py:35
  104.9 12.6 %collective-permute-done.6.top = bf16[32,768]{1,0:T(8,128)(2,1)S(1)} collective-permute-done((bf16[32,768]{1,0:T(8,128)(2,1)S(1)}, bf16[32,768]{1,0:T(8,128)(2,1)S(1)}, u32[]{:S(2)}, u32[]{:S(2)}) %collective-permute-start.6) | collective-permute-done | bytes 49184 | tf_op jit(solution)/shard_map/ppermute | solution.py:34
  118.2 8.2 %all-to-all-start.3 = ((bf16[128,8,128]{2,1,0:T(8,128)(2,1)}), bf16[128,8,128]{2,1,0:T(8,128)(2,1)S(1)}, u32[]{:S(2)}, u32[]{:S(2)}) async-start(bf16[128,8,128]{2,1,0:T(8,128)(2,1)} %copy-done.18), calls=%async_computation.3 | async-start | bytes 524288 | tf_op jit(solution)/shard_map/all_to_all | solution.py:495
  129.5 8.2 %all-to-all-done.3.blocks = bf16[128,8,128]{2,1,0:T(8,128)(2,1)S(1)} async-done(((bf16[128,8,128]{2,1,0:T(8,128)(2,1)}), bf16[128,8,128]{2,1,0:T(8,128)(2,1)S(1)}, u32[]{:S(2)}, u32[]{:S(2)}) %all-to-all-start.3) | async-done | bytes 262176 | tf_op jit(solution)/shard_map/all_to_all | solution.py:495
  137.6 1.8 %pieces.1 = (bf16[16,24,384]{2,1,0:T(8,128)(2,1)S(1)}, f32[8,128]{1,0:T(8,128)S(1)}) custom-call(s32[6]{0:T(128)S(1)} %pad_add_fusion.flags, bf16[64,24,384]{2,1,0:T(8,128)(2,1)} %all-to-all-done.2.got, bf16[128,8,128]{2,1,0:T(8,128)(2,1)S(1)} %all-to-all-done.3.blocks, bf16[4,128,384]{2,1,0:T(8,128)(2,1)S(1)} %pad_maximum_fusion.near, ...), custom_call_target="tpu_custom_call" | custom-call | flops 100000000 | bytes 2500000 | tf_op jit(solution)/shard_map/pieces/pallas_call | solution.py:383
  140.2 5.4 %all-to-all-start.4 = ((bf16[16,24,384]{2,1,0:T(8,128)(2,1)}), bf16[16,24,384]{2,1,0:T(8,128)(2,1)S(1)}, u32[]{:S(2)}, u32[]{:S(2)}) async-start(bf16[16,24,384]{2,1,0:T(8,128)(2,1)} %copy-done.17), calls=%async_computation.4 | async-start | bytes 589824 | tf_op jit(solution)/shard_map/all_to_all | solution.py:512
  147.2 3.3 %unmix.1 = bf16[16,32,768]{2,1,0:T(8,128)(2,1)} custom-call(s32[6]{0:T(128)S(1)} %pad_add_fusion.flags, f32[16,32,768]{2,1,0:T(8,128)S(1)} %bitcast.64, f32[8,768]{1,0:T(8,128)S(1)} %copy-done.26, bf16[32,768]{1,0:T(8,128)(2,1)S(1)} %collective-permute-done.6.top, bf16[32,768]{1,0:T(8,128)(2,1)S(1)} %copy-done.24, ...), custom_call_target="tpu_custom_call" | custom-call | flops 8000000 | bytes 3000000 | tf_op jit(solution)/shard_map/unmix/pallas_call | solution.py:421
  151.3 1.4 all-to-all-done.4
  (128 shorter events, 27.8 us)
Async XLA Ops:
  0.6 31.2 %copy-start = (bf16[768,768]{1,0:T(8,128)(2,1)S(1)}, bf16[768,768]{1,0:T(8,128)(2,1)}, u32[]{:S(2)}) copy-start(bf16[768,768]{1,0:T(8,128)(2,1)} %param.9) | copy-start | bytes 3538948
  1.6 9.4 %collective-permute-start = (bf16[32,768]{1,0:T(8,128)(2,1)S(1)}, bf16[32,768]{1,0:T(8,128)(2,1)S(1)}, u32[]{:S(2)}, u32[]{:S(2)}) collective-permute-start(bf16[32,768]{1,0:T(8,128)(2,1)S(1)} %get-tuple-element.48), channel_id=1, source_target_pairs={{0,16},{16,32},{32,48},{48,64},{64,80},{80,96},{96,112},{112,0},{1... | collective-permute-start | bytes 147464 | tf_op jit(solution)/shard_map/ppermute | solution.py:34
  4.1 6.9 %collective-permute-start.1 = (bf16[32,768]{1,0:T(8,128)(2,1)S(1)}, bf16[32,768]{1,0:T(8,128)(2,1)S(1)}, u32[]{:S(2)}, u32[]{:S(2)}) collective-permute-start(bf16[32,768]{1,0:T(8,128)(2,1)S(1)} %get-tuple-element.47), channel_id=1, source_target_pairs={{16,0},{32,16},{48,32},{64,48},{80,64},{96,80},{112,96},{0,112},{1... | collective-permute-start | bytes 147464 | tf_op jit(solution)/shard_map/ppermute | solution.py:35
  7.5 8.1 %copy-start.2 = (bf16[16,32,768]{2,1,0:T(8,128)(2,1)S(1)}, bf16[16,32,768]{2,1,0:T(8,128)(2,1)}, u32[]{:S(2)}) copy-start(bf16[16,32,768]{2,1,0:T(8,128)(2,1)} %image.3) | copy-start | bytes 2359300
  7.5 8.1 %copy-start.21 = (f32[9,768]{1,0:T(8,128)S(1)}, f32[9,768]{1,0:T(8,128)}, u32[]{:S(2)}) copy-start(f32[9,768]{1,0:T(8,128)} %taps.3) | copy-start | bytes 82948
  11.0 22.5 %copy-start.9 = (bf16[32,768]{1,0:T(8,128)(2,1)}, bf16[32,768]{1,0:T(8,128)(2,1)S(1)}, u32[]{:S(2)}) copy-start(bf16[32,768]{1,0:T(8,128)(2,1)S(1)} %collective-permute-done.top) | copy-start | bytes 147460
  11.0 22.4 %copy-start.11 = (bf16[32,768]{1,0:T(8,128)(2,1)}, bf16[32,768]{1,0:T(8,128)(2,1)S(1)}, u32[]{:S(2)}) copy-start(bf16[32,768]{1,0:T(8,128)(2,1)S(1)} %collective-permute-done.1.bottom) | copy-start | bytes 147460
  11.1 2.4 %collective-permute-start.2 = (bf16[18,768]{1,0:T(8,128)(2,1)S(1)}, bf16[18,768]{1,0:T(8,128)(2,1)S(1)}, u32[]{:S(2)}, u32[]{:S(2)}) collective-permute-start(bf16[18,768]{1,0:T(8,128)(2,1)S(1)} %get-tuple-element.56), channel_id=1, source_target_pairs={{0,1},{1,0},{2,3},{3,2},{4,5},{5,4},{6,7},{7,6},{8,9},{9,8},{10,11... | collective-permute-start | bytes 82952 | tf_op jit(solution)/shard_map/ppermute | solution.py:41
  12.1 3.4 %collective-permute-start.3 = (bf16[18,768]{1,0:T(8,128)(2,1)S(1)}, bf16[18,768]{1,0:T(8,128)(2,1)S(1)}, u32[]{:S(2)}, u32[]{:S(2)}) collective-permute-start(bf16[18,768]{1,0:T(8,128)(2,1)S(1)} %get-tuple-element.55), channel_id=1, source_target_pairs={{0,15},{1,2},{2,1},{3,4},{4,3},{5,6},{6,5},{7,8},{8,7},{9,10},{10,... | collective-permute-start | bytes 82952 | tf_op jit(solution)/shard_map/ppermute | solution.py:42
  15.5 3.7 %copy-start.15 = (bf16[18,768]{1,0:T(8,128)(2,1)}, bf16[18,768]{1,0:T(8,128)(2,1)S(1)}, u32[]{:S(2)}) copy-start(bf16[18,768]{1,0:T(8,128)(2,1)S(1)} %get-tuple-element.52.left) | copy-start | bytes 82948
  20.5 13.0 %copy-start.7 = (bf16[512,768]{1,0:T(8,128)(2,1)}, bf16[512,768]{1,0:T(8,128)(2,1)S(1)}, u32[]{:S(2)}) copy-start(bf16[512,768]{1,0:T(8,128)(2,1)S(1)} %get-tuple-element.22) | copy-start | bytes 2359300
  20.5 19.4 %all-to-all-start = ((bf16[16,8,768]{2,1,0:T(8,128)(2,1)}), bf16[16,8,768]{2,1,0:T(8,128)(2,1)S(1)}, u32[]{:S(2)}, u32[]{:S(2)}) async-start(bf16[16,8,768]{2,1,0:T(8,128)(2,1)} %get-tuple-element.23), calls=%async_computation | async-start | bytes 393216 | tf_op jit(solution)/shard_map/all_to_all | solution.py:461
  52.3 2.6 %copy-start.33 = (bf16[768,512]{1,0:T(8,128)(2,1)S(1)}, bf16[768,512]{1,0:T(8,128)(2,1)}, u32[]{:S(2)}) copy-start(bf16[768,512]{1,0:T(8,128)(2,1)} %get-tuple-element.25) | copy-start | bytes 2359300
  54.3 25.3 %collective-permute-start.4 = (bf16[768,384]{1,0:T(8,128)(2,1)}, bf16[768,384]{1,0:T(8,128)(2,1)}, u32[]{:S(2)}, u32[]{:S(2)}) collective-permute-start(bf16[768,384]{1,0:T(8,128)(2,1)} %convolution_convert_fusion.3), channel_id=1, source_target_pairs={{0,1},{1,0},{2,3},{3,2},{4,5},{5,4},{6,7},{7,6},{8,9},{9,8},{10,11... | collective-permute-start | bytes 1769480 | tf_op jit(solution)/shard_map/ppermute | solution.py:481
  56.3 23.3 %collective-permute-start.5 = (bf16[768,384]{1,0:T(8,128)(2,1)}, bf16[768,384]{1,0:T(8,128)(2,1)}, u32[]{:S(2)}, u32[]{:S(2)}) collective-permute-start(bf16[768,384]{1,0:T(8,128)(2,1)} %fusion.1), channel_id=1, source_target_pairs={{0,1},{1,0},{2,3},{3,2},{4,5},{5,4},{6,7},{7,6},{8,9},{9,8},{10,11... | collective-permute-start | bytes 1769480 | tf_op jit(solution)/shard_map/ppermute | solution.py:481
  56.3 13.3 %collective-permute-start.10 = (bf16[1,128,384]{2,1,0:T(8,128)(2,1)}, bf16[1,128,384]{2,1,0:T(8,128)(2,1)}, u32[]{:S(2)}, u32[]{:S(2)}) collective-permute-start(bf16[1,128,384]{2,1,0:T(8,128)(2,1)} %dynamic-slice_bitcast_fusion), channel_id=1, source_target_pairs={{0,16},{16,0},{32,48},{48,32},{64,80},{80,64},{96,112},{112,96},{1... | collective-permute-start | bytes 294920 | tf_op jit(solution)/shard_map/ppermute | solution.py:466
  57.8 24.4 %all-to-all-start.1 = ((bf16[16,2,8,768]{3,2,1,0:T(8,128)(2,1)}), bf16[16,2,8,768]{3,2,1,0:T(8,128)(2,1)}, u32[]{:S(2)}, u32[]{:S(2)}) async-start(bf16[16,2,8,768]{3,2,1,0:T(8,128)(2,1)} %get-tuple-element.28), calls=%async_computation.1 | async-start | bytes 786432 | tf_op jit(solution)/shard_map/all_to_all | solution.py:470
  69.6 10.1 %copy-start.3 = (bf16[768,384]{1,0:T(8,128)(2,1)S(1)}, bf16[768,384]{1,0:T(8,128)(2,1)}, u32[]{:S(2)}) copy-start(bf16[768,384]{1,0:T(8,128)(2,1)} %convolution_convert_fusion.5.own_query) | copy-start | bytes 1769476
  69.6 10.1 %copy-start.4 = (bf16[768,384]{1,0:T(8,128)(2,1)S(1)}, bf16[768,384]{1,0:T(8,128)(2,1)}, u32[]{:S(2)}) copy-start(bf16[768,384]{1,0:T(8,128)(2,1)} %fusion.own_out) | copy-start | bytes 1769476
  70.7 6.3 %collective-permute-start.11 = (bf16[2,128,384]{2,1,0:T(8,128)(2,1)S(1)}, bf16[2,128,384]{2,1,0:T(8,128)(2,1)S(1)}, u32[]{:S(2)}, u32[]{:S(2)}) collective-permute-start(bf16[2,128,384]{2,1,0:T(8,128)(2,1)S(1)} %pad_maximum_fusion.1), channel_id=1, source_target_pairs={{0,32},{16,48},{32,0},{48,16},{64,96},{80,112},{96,64},{112,80},{1... | collective-permute-start | bytes 589832 | tf_op jit(solution)/shard_map/ppermute | solution.py:466
  77.9 51.6 %collective-permute-start.12 = (bf16[4,128,384]{2,1,0:T(8,128)(2,1)S(1)}, bf16[4,128,384]{2,1,0:T(8,128)(2,1)}, u32[]{:S(2)}, u32[]{:S(2)}) collective-permute-start(bf16[4,128,384]{2,1,0:T(8,128)(2,1)S(1)} %pad_maximum_fusion.near), channel_id=1, source_target_pairs={{0,64},{16,80},{32,96},{48,112},{64,0},{80,16},{96,32},{112,48},{1... | collective-permute-start | bytes 1179656 | tf_op jit(solution)/shard_map/ppermute | solution.py:466
  90.6 14.2 %copy-start.37 = (f32[16,1,768]{2,1,0:T(1,128)S(1)}, f32[16,1,768]{2,1,0:T(1,128)}, u32[]{:S(2)}) copy-start(f32[16,1,768]{2,1,0:T(1,128)} %get-tuple-element.41) | copy-start | bytes 147460
  90.6 14.2 %copy-start.36 = (f32[16,1,768]{2,1,0:T(1,128)S(1)}, f32[16,1,768]{2,1,0:T(1,128)}, u32[]{:S(2)}) copy-start(f32[16,1,768]{2,1,0:T(1,128)} %get-tuple-element.42) | copy-start | bytes 147460
  90.6 27.5 %all-to-all-start.2 = ((bf16[64,24,384]{2,1,0:T(8,128)(2,1)}), bf16[64,24,384]{2,1,0:T(8,128)(2,1)}, u32[]{:S(2)}, u32[]{:S(2)}) async-start(bf16[64,24,384]{2,1,0:T(8,128)(2,1)} %bitcast.65), calls=%async_computation.2 | async-start | bytes 2359296 | tf_op jit(solution)/shard_map/all_to_all | solution.py:485
  101.2 16.3 %collective-permute-start.6 = (bf16[32,768]{1,0:T(8,128)(2,1)S(1)}, bf16[32,768]{1,0:T(8,128)(2,1)S(1)}, u32[]{:S(2)}, u32[]{:S(2)}) collective-permute-start(bf16[32,768]{1,0:T(8,128)(2,1)S(1)} %get-tuple-element.44), channel_id=1, source_target_pairs={{0,16},{16,32},{32,48},{48,64},{64,80},{80,96},{96,112},{112,0},{1... | collective-permute-start | bytes 147464 | tf_op jit(solution)/shard_map/ppermute | solution.py:34
  102.4 15.1 %collective-permute-start.7 = (bf16[32,768]{1,0:T(8,128)(2,1)S(1)}, bf16[32,768]{1,0:T(8,128)(2,1)S(1)}, u32[]{:S(2)}, u32[]{:S(2)}) collective-permute-start(bf16[32,768]{1,0:T(8,128)(2,1)S(1)} %get-tuple-element.43), channel_id=1, source_target_pairs={{16,0},{32,16},{48,32},{64,48},{80,64},{96,80},{112,96},{0,112},{1... | collective-permute-start | bytes 147464 | tf_op jit(solution)/shard_map/ppermute | solution.py:35
  118.2 19.5 %all-to-all-start.3 = ((bf16[128,8,128]{2,1,0:T(8,128)(2,1)}), bf16[128,8,128]{2,1,0:T(8,128)(2,1)S(1)}, u32[]{:S(2)}, u32[]{:S(2)}) async-start(bf16[128,8,128]{2,1,0:T(8,128)(2,1)} %copy-done.18), calls=%async_computation.3 | async-start | bytes 524288 | tf_op jit(solution)/shard_map/all_to_all | solution.py:495
  127.7 17.9 %collective-permute-start.8 = (bf16[18,768]{1,0:T(8,128)(2,1)}, bf16[18,768]{1,0:T(8,128)(2,1)}, u32[]{:S(2)}, u32[]{:S(2)}) collective-permute-start(bf16[18,768]{1,0:T(8,128)(2,1)} %get-tuple-element.54), channel_id=1, source_target_pairs={{0,1},{1,0},{2,3},{3,2},{4,5},{5,4},{6,7},{7,6},{8,9},{9,8},{10,11... | collective-permute-start | bytes 82952 | tf_op jit(solution)/shard_map/ppermute | solution.py:41
  128.8 17.6 %copy-start.22 = (f32[9,768]{1,0:T(8,128)S(1)}, f32[9,768]{1,0:T(8,128)}, u32[]{:S(2)}) copy-start(f32[9,768]{1,0:T(8,128)} %taps.3) | copy-start | bytes 82948
  128.8 17.6 %copy-start.26 = (f32[8,768]{1,0:T(8,128)S(1)}, f32[8,768]{1,0:T(8,128)}, u32[]{:S(2)}) copy-start(f32[8,768]{1,0:T(8,128)} %copy-done.25) | copy-start | bytes 73732
  128.8 16.8 %collective-permute-start.9 = (bf16[18,768]{1,0:T(8,128)(2,1)}, bf16[18,768]{1,0:T(8,128)(2,1)}, u32[]{:S(2)}, u32[]{:S(2)}) collective-permute-start(bf16[18,768]{1,0:T(8,128)(2,1)} %get-tuple-element.53), channel_id=1, source_target_pairs={{0,15},{1,2},{2,1},{3,4},{4,3},{5,6},{6,5},{7,8},{8,7},{9,10},{10,... | collective-permute-start | bytes 82952 | tf_op jit(solution)/shard_map/ppermute | solution.py:42
  140.2 12.5 %all-to-all-start.4 = ((bf16[16,24,384]{2,1,0:T(8,128)(2,1)}), bf16[16,24,384]{2,1,0:T(8,128)(2,1)S(1)}, u32[]{:S(2)}, u32[]{:S(2)}) async-start(bf16[16,24,384]{2,1,0:T(8,128)(2,1)} %copy-done.17), calls=%async_computation.4 | async-start | bytes 589824 | tf_op jit(solution)/shard_map/all_to_all | solution.py:512
  (24 other events, 24.6 us)

commit v2 on v1

--- a/solution.py
+++ b/solution.py
@@ -11,7 +11,7 @@
 BF = jnp.bfloat16
 F32 = jnp.float32
 LANES = 128
-WIDE = 256
+WIDE = 768
 
 FINAL = (0, 1, 2, 3, 12, 13, 14, 15)
 PARTNER = (5, 4, 7, 6, 9, 8, 11, 10)
@@ -176,6 +176,21 @@
 
 
 def attend_kernel(query, dout, cells, w_key, w_value, attended, grad_query, sums):
+    for pair in range(query.shape[1] // LANES):
+        at = pl.ds(pair * LANES, LANES)
+        attend_pair(
+            query.at[:, at],
+            dout.at[:, at],
+            cells,
+            w_key.at[:, at],
+            w_value.at[:, at],
+            attended.at[at],
+            grad_query.at[at],
+            sums.at[:, :, :, at],
+        )
+
+
+def attend_pair(query, dout, cells, w_key, w_value, attended, grad_query, sums):
     low = lax.broadcasted_iota(jnp.int32, (128, LANES), 1) < HD
     all_cells = cells[...]
     zero = jnp.zeros((128, LANES), BF)
@@ -211,12 +226,12 @@
 
 def attend(query, dout, cells, w_key, w_value):
     tokens, channels = query.shape
-    by_pair = pl.BlockSpec((tokens, LANES), lambda i: (0, i))
-    turned = pl.BlockSpec((LANES, tokens), lambda i: (i, 0))
-    weight = pl.BlockSpec((channels, LANES), lambda i: (0, i))
+    by_pair = pl.BlockSpec((tokens, 384), lambda i: (0, i))
+    turned = pl.BlockSpec((384, tokens), lambda i: (i, 0))
+    weight = pl.BlockSpec((channels, 384), lambda i: (0, i))
     return pl.pallas_call(
         attend_kernel,
-        grid=(channels // LANES,),
+        grid=(channels // 384,),
         in_specs=[
             by_pair,
             by_pair,
@@ -224,7 +239,7 @@
             weight,
             weight,
         ],
-        out_specs=[turned, turned, pl.BlockSpec((16, 2, 8, LANES), lambda i: (0, 0, 0, i))],
+        out_specs=[turned, turned, pl.BlockSpec((16, 2, 8, 384), lambda i: (0, 0, 0, i))],
         out_shape=[
             jax.ShapeDtypeStruct((channels, tokens), BF),
             jax.ShapeDtypeStruct((channels, tokens), BF),
@@ -360,8 +375,22 @@
     )(terms, w_key, w_value, standard, inverse, early, windows)
 
 
-def pieces_kernel(flags, got, blocks, near, far, placed, conv):
-    piece = jnp.sum(got[...].astype(F32), axis=0).astype(BF)
+def sum_kernel(got, total):
+    total[...] = jnp.sum(got[...].astype(F32), axis=0).astype(BF)
+
+
+def summed(got):
+    return pl.pallas_call(
+        sum_kernel,
+        out_shape=jax.ShapeDtypeStruct(got.shape[1:], BF),
+        compiler_params=pltpu.CompilerParams(vmem_limit_bytes=16 << 20),
+        cost_estimate=pl.CostEstimate(flops=600_000, bytes_accessed=1_200_000, transcendentals=0),
+        name="summed",
+    )(got)
+
+
+def pieces_kernel(flags, own, blocks, near, far, placed, conv):
+    piece = own[...]
     conv[...] = jnp.sum(blocks[...].astype(F32), axis=0)
     total = jnp.zeros((LANES, piece.shape[1]), F32)
     for i in range(8):
@@ -377,7 +406,7 @@
         placed[8 + q] = second
 
 
-def pieces(flags, got, blocks, near, far):
+def pieces(flags, piece, blocks, near, far):
     half = near.shape[2]
     vmem = pl.BlockSpec(memory_space=pltpu.VMEM)
     return pl.pallas_call(
@@ -390,7 +419,7 @@
         compiler_params=pltpu.CompilerParams(vmem_limit_bytes=16 << 20),
         cost_estimate=pl.CostEstimate(flops=100_000_000, bytes_accessed=2_500_000, transcendentals=0),
         name="pieces",
-    )(flags, got, blocks, near, far)
+    )(flags, piece, blocks, near, far)
 
 
 def unmix_kernel(flags, early, pooled, top, bottom, left, right, taps, image, padded):
@@ -481,7 +510,6 @@
     theirs = [lax.ppermute(x, "col", PAIRS) for x in sent]
     own = lax.optimization_barrier(half_terms(core))
     chip = chip_sums(own, theirs)
-    chip, terms = lax.optimization_barrier((chip, terms))
     got = lax.all_to_all(
         chip.reshape(64, 24, half), BOTH, 0, 0, tiled=True, axis_index_groups=SUM_GROUPS
     )
@@ -508,7 +536,8 @@
         jnp.concatenate([over[-1:], last, under[-1:]], axis=0),
     )
     grad_image = unmix(flags, early, pooled, (top, bottom, left, right), conv_taps)
-    placed, conv = pieces(flags, got, blocks, near, far)
+    piece = summed(got)
+    placed, conv = pieces(flags, piece, blocks, near, far)
     placed = lax.all_to_all(
         placed, BOTH, 0, 0, tiled=True, axis_index_groups=PLACE_GROUPS
     )

time: 155 us -> 153 us (0.987)
  local copies, waits for them, and re-layouts: 20.5 us -> 18.7 us
  waiting for transfers between devices: 36 us -> 34.3 us
    all_to_all x1, waiting for transfers between devices: 0.01 us -> 13.2 us  [block_gradients(): lax.all_to_all(chip.reshape(64, 24, half), BOTH, 0, 0, tiled=True, axis_i...]
    ppermute x2, waiting for transfers between devices: 12.6 us -> 0.01 us  [from_both_sides(): lax.ppermute(last, axis, [(i, (i + 1) % count) for i in range(count)])]
    all_to_all x1, starting transfers between devices: 8.16 us -> 10.3 us  [block_gradients(): blocks = lax.all_to_all(block, BOTH, 0, 0, tiled=True)]
    all_to_all x1, starting transfers between devices: 10.5 us -> 8.64 us  [block_gradients(): lax.all_to_all(chip.reshape(64, 24, half), BOTH, 0, 0, tiled=True, axis_i...]
    unnamed x76, local copies, waits for them, and re-layouts: 15.3 us -> 13.4 us
    pallas_call x1 -> x2, Pallas kernels: 7.92 us -> 8.65 us  [the longest x1 7.19 us: attend(): pl.pallas_call(attend_kernel, grid=(channels // 384,), in_specs=[by_pair,...]
where the time goes in v2:
time: 153 us; the launch traced here: 151 us
  starting transfers between devices  54.9 us (36%)
  waiting for transfers between devices  34.3 us (22%)
  Pallas kernels  23.3 us (15%)
  local copies, waits for them, and re-layouts  18.7 us (12%)
  matrix products  13 us (8%)
  other arithmetic  5.7 us (4%)
    unnamed x76, local copies, waits for them, and re-layouts  13.4 us
    all_to_all x1, waiting for transfers between devices, block_gradients(): lax.all_to_all(chip.reshape(64, 24, half), BOTH, 0, 0, tiled=True, axis_i...  13.2 us
    dot_general x6, matrix products, dot(): lax.dot_general(left, right, ((dims[0], dims[1]), ((), ())), preferred_el...  11.3 us
    all_to_all x1, starting transfers between devices, block_gradients(): cells = lax.all_to_all(normed, 'col', 0, 0, tiled=True)  11.3 us
    all_to_all x1, starting transfers between devices, block_gradients(): blocks = lax.all_to_all(block, BOTH, 0, 0, tiled=True)  10.3 us
    all_to_all x1, starting transfers between devices, block_gradients(): lax.all_to_all(chip.reshape(64, 24, half), BOTH, 0, 0, tiled=True, axis_i...  8.64 us
    pallas_call x1, Pallas kernels, attend(): pl.pallas_call(attend_kernel, grid=(channels // 384,), in_specs=[by_pair,...  7.19 us
    all_to_all x1, waiting for transfers between devices, block_gradients(): blocks = lax.all_to_all(block, BOTH, 0, 0, tiled=True)  6.69 us
  transfers between devices with their start and end apart: 18, of which 6 were waited for; matrix products, arithmetic and copies ran while one was open for 10% of the time, Pallas kernels for 8%

profile of v2, /device:TPU:1, one launch (start us, length us, event | category | flops | bytes accessed | tf_op | source)
XLA Modules:
  0.0 151.1 jit_solution(18409190675002785944)
XLA Ops:
  1.6 2.5 %collective-permute-start = (bf16[32,768]{1,0:T(8,128)(2,1)S(1)}, bf16[32,768]{1,0:T(8,128)(2,1)S(1)}, u32[]{:S(2)}, u32[]{:S(2)}) collective-permute-start(bf16[32,768]{1,0:T(8,128)(2,1)S(1)} %get-tuple-element.44), channel_id=1, source_target_pairs={{0,16},{16,32},{32,48},{48,64},{64,80},{80,96},{96,112},{112,0},{1... | collective-permute-start | bytes 147464 | tf_op jit(solution)/shard_map/ppermute | solution.py:34
  4.1 2.3 %collective-permute-start.1 = (bf16[32,768]{1,0:T(8,128)(2,1)S(1)}, bf16[32,768]{1,0:T(8,128)(2,1)S(1)}, u32[]{:S(2)}, u32[]{:S(2)}) collective-permute-start(bf16[32,768]{1,0:T(8,128)(2,1)S(1)} %get-tuple-element.43), channel_id=1, source_target_pairs={{16,0},{32,16},{48,32},{64,48},{80,64},{96,80},{112,96},{0,112},{1... | collective-permute-start | bytes 147464 | tf_op jit(solution)/shard_map/ppermute | solution.py:35
  7.5 3.3 %convolution_convert_fusion.dout = bf16[512,768]{1,0:T(8,128)(2,1)} fusion(bf16[512,768]{1,0:T(8,128)(2,1)} %bitcast.66, bf16[768,768]{1,0:T(8,128)(2,1)} %param.12), kind=kOutput, calls=%fused_computation.1 | convolution fusion | flops 604372992 | bytes 2752512 | tf_op jit(solution)/shard_map/dot_general | solution.py:57
  12.1 1.3 collective-permute-start.3
  13.5 2.0 %collective-permute-done.3 = bf16[18,768]{1,0:T(8,128)(2,1)S(1)} collective-permute-done((bf16[18,768]{1,0:T(8,128)(2,1)S(1)}, bf16[18,768]{1,0:T(8,128)(2,1)S(1)}, u32[]{:S(2)}, u32[]{:S(2)}) %collective-permute-start.3) | collective-permute-done | bytes 27680 | tf_op jit(solution)/shard_map/ppermute | solution.py:42
  15.6 3.5 %mix.1 = (bf16[512,768]{1,0:T(8,128)(2,1)S(1)}, f32[8,768]{1,0:T(8,128)S(1)}, f32[8,128]{1,0:T(8,128)S(1)}, bf16[16,8,768]{2,1,0:T(8,128)(2,1)}) custom-call(s32[6]{0:T(128)S(1)} %pad_add_fusion.flags, bf16[16,32,768]{2,1,0:T(8,128)(2,1)S(1)} %copy-done.2, bf16[32,768]{1,0:T(8,128)(2,1)S(1)} %collective-permute-done.top, ...), custom_call_target="tpu_custom_call" | custom-call | flops 8000000 | bytes 2000000 | tf_op jit(solution)/shard_map/mix/pallas_call | solution.py:147
  20.3 11.3 %all-to-all-start = ((bf16[16,8,768]{2,1,0:T(8,128)(2,1)}), bf16[16,8,768]{2,1,0:T(8,128)(2,1)S(1)}, u32[]{:S(2)}, u32[]{:S(2)}) async-start(bf16[16,8,768]{2,1,0:T(8,128)(2,1)} %get-tuple-element.21), calls=%async_computation | async-start | bytes 393216 | tf_op jit(solution)/shard_map/all_to_all | solution.py:490
  31.6 1.7 %convolution_convert_fusion.1.query = bf16[512,768]{1,0:T(8,128)(2,1)} fusion(bf16[512,768]{1,0:T(8,128)(2,1)S(1)} %get-tuple-element.20, bf16[768,768]{1,0:T(8,128)(2,1)S(1)} %copy-done), kind=kOutput, calls=%fused_computation.2 | convolution fusion | flops 604372992 | bytes 2752512 | tf_op jit(solution)/shard_map/dot_general | solution.py:492
  33.2 6.4 %all-to-all-done = bf16[16,8,768]{2,1,0:T(8,128)(2,1)S(1)} async-done(((bf16[16,8,768]{2,1,0:T(8,128)(2,1)}), bf16[16,8,768]{2,1,0:T(8,128)(2,1)S(1)}, u32[]{:S(2)}, u32[]{:S(2)}) %all-to-all-start) | async-done | bytes 196640 | tf_op jit(solution)/shard_map/all_to_all | solution.py:490
  40.4 7.2 %attend.1 = (bf16[768,512]{1,0:T(8,128)(2,1)}, bf16[768,512]{1,0:T(8,128)(2,1)}, bf16[16,2,8,768]{3,2,1,0:T(8,128)(2,1)}) custom-call(bf16[512,768]{1,0:T(8,128)(2,1)} %convolution_convert_fusion.1.query, bf16[512,768]{1,0:T(8,128)(2,1)} %convolution_convert_fusion.dout, bf16[128,768]{1,0:T(8,128)(2,1)} %bitcast.72, bf16[768,768]{1,0:T(8,128)(2,1)} %w_key.3, ...), custom_call_target="tpu_custom_call" | custom-call | flops 3000000000 | bytes 6000000 | tf_op jit(solution)/shard_map/attend/pallas_call | solution.py:232
  47.6 2.3 %convert_add_fusion = f32[512,768]{1,0:T(8,128)S(1)} fusion(bf16[512,768]{1,0:T(8,128)(2,1)} %bitcast.67, bf16[768,512]{1,0:T(8,128)(2,1)} %get-tuple-element.22, bf16[768,768]{1,0:T(8,128)(2,1)S(1)} %copy-done), kind=kOutput, calls=%fused_computation | convolution fusion | flops 604766208 | bytes 4325376 | tf_op jit(solution)/shard_map/dot_general | solution.py:57
  50.0 1.4 convolution_convert_fusion.5.own_query
  52.0 1.5 fusion.own_out
  53.5 1.4 convolution_convert_fusion.3
  54.9 1.4 fusion.1
  56.9 4.5 %all-to-all-start.1 = ((bf16[16,2,8,768]{3,2,1,0:T(8,128)(2,1)}), bf16[16,2,8,768]{3,2,1,0:T(8,128)(2,1)}, u32[]{:S(2)}, u32[]{:S(2)}) async-start(bf16[16,2,8,768]{3,2,1,0:T(8,128)(2,1)} %get-tuple-element.23), calls=%async_computation.1 | async-start | bytes 786432 | tf_op jit(solution)/shard_map/all_to_all | solution.py:499
  64.5 2.8 %tap_terms.1 = (f32[9,768]{1,0:T(8,128)S(1)}, f32[9,8,768]{2,1,0:T(8,128)S(1)}) custom-call(s32[6]{0:T(128)S(1)} %pad_add_fusion.flags, bf16[16,32,768]{2,1,0:T(8,128)(2,1)S(1)} %copy-done.2, bf16[32,768]{1,0:T(8,128)(2,1)S(1)} %copy-done.10, bf16[32,768]{1,0:T(8,128)(2,1)S(1)} %copy-done.12, bf16[18,768]{1,0:T(8,128)(2,1)S(1)} %copy-done.16, ...), custom_call_target="tpu_custom_call" | custom-call | flops 8000000 | bytes 3000000 | tf_op jit(solution)/shard_map/tap_terms/pallas_call | solution.py:309
  69.3 5.2 %collective-permute-done.11 = bf16[2,128,384]{2,1,0:T(8,128)(2,1)S(1)} collective-permute-done((bf16[2,128,384]{2,1,0:T(8,128)(2,1)S(1)}, bf16[2,128,384]{2,1,0:T(8,128)(2,1)S(1)}, u32[]{:S(2)}, u32[]{:S(2)}) %collective-permute-start.11) | collective-permute-done | bytes 196640 | tf_op jit(solution)/shard_map/ppermute | solution.py:495
  75.5 1.7 %collective-permute-start.12 = (bf16[4,128,384]{2,1,0:T(8,128)(2,1)S(1)}, bf16[4,128,384]{2,1,0:T(8,128)(2,1)}, u32[]{:S(2)}, u32[]{:S(2)}) collective-permute-start(bf16[4,128,384]{2,1,0:T(8,128)(2,1)S(1)} %pad_maximum_fusion.near), channel_id=1, source_target_pairs={{0,64},{16,80},{32,96},{48,112},{64,0},{80,16},{96,32},{112,48},{1... | collective-permute-start | bytes 1179656 | tf_op jit(solution)/shard_map/ppermute | solution.py:495
  77.2 1.3 copy-done.5
  82.2 2.2 %at_cells.1 = (f32[8,768]{1,0:T(8,128)S(1)}, bf16[128,8,128]{2,1,0:T(8,128)(2,1)S(1)}) custom-call(bf16[16,2,8,768]{3,2,1,0:T(8,128)(2,1)} %all-to-all-done.1.terms, bf16[768,768]{1,0:T(8,128)(2,1)S(1)} %copy-done.5, bf16[768,768]{1,0:T(8,128)(2,1)S(1)} %copy-done.6, f32[8,768]{1,0:T(8,128)S(1)} %copy-done.30, f32[8,128]{1,0:T(8,128)S(1)} %get-tuple-element.25.inverse, ...), custom_call_target="tpu_custom_call" | custom-call | flops 30000000 | bytes 3500000 | tf_op jit(solution)/shard_map/at_cells/pallas_call | solution.py:366
  85.1 1.6 %collective-permute-start.4 = (bf16[32,768]{1,0:T(8,128)(2,1)}, bf16[32,768]{1,0:T(8,128)(2,1)S(1)}, u32[]{:S(2)}, u32[]{:S(2)}) collective-permute-start(bf16[32,768]{1,0:T(8,128)(2,1)} %get-tuple-element.40), channel_id=1, source_target_pairs={{0,16},{16,32},{32,48},{48,64},{64,80},{80,96},{96,112},{112,0},{1... | collective-permute-start | bytes 147464 | tf_op jit(solution)/shard_map/ppermute | solution.py:34
  86.7 2.0 %collective-permute-start.5 = (bf16[32,768]{1,0:T(8,128)(2,1)}, bf16[32,768]{1,0:T(8,128)(2,1)S(1)}, u32[]{:S(2)}, u32[]{:S(2)}) collective-permute-start(bf16[32,768]{1,0:T(8,128)(2,1)} %get-tuple-element.39), channel_id=1, source_target_pairs={{16,0},{32,16},{48,32},{64,48},{80,64},{96,80},{112,96},{0,112},{1... | collective-permute-start | bytes 147464 | tf_op jit(solution)/shard_map/ppermute | solution.py:35
  88.8 1.5 chip_sums.1
  91.3 8.6 %all-to-all-start.2 = ((bf16[64,24,384]{2,1,0:T(8,128)(2,1)}), bf16[64,24,384]{2,1,0:T(8,128)(2,1)}, u32[]{:S(2)}, u32[]{:S(2)}) async-start(bf16[64,24,384]{2,1,0:T(8,128)(2,1)} %bitcast.65), calls=%async_computation.2 | async-start | bytes 2359296 | tf_op jit(solution)/shard_map/all_to_all | solution.py:513
  100.8 13.2 %all-to-all-done.2.got = bf16[64,24,384]{2,1,0:T(8,128)(2,1)} async-done(((bf16[64,24,384]{2,1,0:T(8,128)(2,1)}), bf16[64,24,384]{2,1,0:T(8,128)(2,1)}, u32[]{:S(2)}, u32[]{:S(2)}) %all-to-all-start.2) | async-done | bytes 1179680 | tf_op jit(solution)/shard_map/all_to_all | solution.py:513
  114.0 10.3 %all-to-all-start.3 = ((bf16[128,8,128]{2,1,0:T(8,128)(2,1)}), bf16[128,8,128]{2,1,0:T(8,128)(2,1)S(1)}, u32[]{:S(2)}, u32[]{:S(2)}) async-start(bf16[128,8,128]{2,1,0:T(8,128)(2,1)} %copy-done.18), calls=%async_computation.3 | async-start | bytes 524288 | tf_op jit(solution)/shard_map/all_to_all | solution.py:523
  127.4 1.5 summed.1.own
  128.9 6.7 %all-to-all-done.3.blocks = bf16[128,8,128]{2,1,0:T(8,128)(2,1)S(1)} async-done(((bf16[128,8,128]{2,1,0:T(8,128)(2,1)}), bf16[128,8,128]{2,1,0:T(8,128)(2,1)S(1)}, u32[]{:S(2)}, u32[]{:S(2)}) %all-to-all-start.3) | async-done | bytes 262176 | tf_op jit(solution)/shard_map/all_to_all | solution.py:523
  135.6 1.4 pieces.1
  137.7 5.4 %all-to-all-start.4 = ((bf16[16,24,384]{2,1,0:T(8,128)(2,1)}), bf16[16,24,384]{2,1,0:T(8,128)(2,1)S(1)}, u32[]{:S(2)}, u32[]{:S(2)}) async-start(bf16[16,24,384]{2,1,0:T(8,128)(2,1)} %copy-done.17), calls=%async_computation.4 | async-start | bytes 589824 | tf_op jit(solution)/shard_map/all_to_all | solution.py:541
  145.5 3.3 %unmix.1 = bf16[16,32,768]{2,1,0:T(8,128)(2,1)} custom-call(s32[6]{0:T(128)S(1)} %pad_add_fusion.flags, f32[16,32,768]{2,1,0:T(8,128)S(1)} %bitcast.64, f32[8,768]{1,0:T(8,128)S(1)} %copy-done.26, bf16[32,768]{1,0:T(8,128)(2,1)S(1)} %collective-permute-done.4.top, bf16[32,768]{1,0:T(8,128)(2,1)S(1)} %copy-done.24, ...), custom_call_target="tpu_custom_call" | custom-call | flops 8000000 | bytes 3000000 | tf_op jit(solution)/shard_map/unmix/pallas_call | solution.py:450
  (129 shorter events, 27.3 us)
Async XLA Ops:
  0.6 30.9 %copy-start = (bf16[768,768]{1,0:T(8,128)(2,1)S(1)}, bf16[768,768]{1,0:T(8,128)(2,1)}, u32[]{:S(2)}) copy-start(bf16[768,768]{1,0:T(8,128)(2,1)} %param.9) | copy-start | bytes 3538948
  1.6 9.4 %collective-permute-start = (bf16[32,768]{1,0:T(8,128)(2,1)S(1)}, bf16[32,768]{1,0:T(8,128)(2,1)S(1)}, u32[]{:S(2)}, u32[]{:S(2)}) collective-permute-start(bf16[32,768]{1,0:T(8,128)(2,1)S(1)} %get-tuple-element.44), channel_id=1, source_target_pairs={{0,16},{16,32},{32,48},{48,64},{64,80},{80,96},{96,112},{112,0},{1... | collective-permute-start | bytes 147464 | tf_op jit(solution)/shard_map/ppermute | solution.py:34
  4.1 6.9 %collective-permute-start.1 = (bf16[32,768]{1,0:T(8,128)(2,1)S(1)}, bf16[32,768]{1,0:T(8,128)(2,1)S(1)}, u32[]{:S(2)}, u32[]{:S(2)}) collective-permute-start(bf16[32,768]{1,0:T(8,128)(2,1)S(1)} %get-tuple-element.43), channel_id=1, source_target_pairs={{16,0},{32,16},{48,32},{64,48},{80,64},{96,80},{112,96},{0,112},{1... | collective-permute-start | bytes 147464 | tf_op jit(solution)/shard_map/ppermute | solution.py:35
  7.5 8.1 %copy-start.2 = (bf16[16,32,768]{2,1,0:T(8,128)(2,1)S(1)}, bf16[16,32,768]{2,1,0:T(8,128)(2,1)}, u32[]{:S(2)}) copy-start(bf16[16,32,768]{2,1,0:T(8,128)(2,1)} %image.3) | copy-start | bytes 2359300
  7.5 8.1 %copy-start.21 = (f32[9,768]{1,0:T(8,128)S(1)}, f32[9,768]{1,0:T(8,128)}, u32[]{:S(2)}) copy-start(f32[9,768]{1,0:T(8,128)} %taps.3) | copy-start | bytes 82948
  11.0 22.3 %copy-start.9 = (bf16[32,768]{1,0:T(8,128)(2,1)}, bf16[32,768]{1,0:T(8,128)(2,1)S(1)}, u32[]{:S(2)}) copy-start(bf16[32,768]{1,0:T(8,128)(2,1)S(1)} %collective-permute-done.top) | copy-start | bytes 147460
  11.0 22.2 %copy-start.11 = (bf16[32,768]{1,0:T(8,128)(2,1)}, bf16[32,768]{1,0:T(8,128)(2,1)S(1)}, u32[]{:S(2)}) copy-start(bf16[32,768]{1,0:T(8,128)(2,1)S(1)} %collective-permute-done.1.bottom) | copy-start | bytes 147460
  11.1 2.4 %collective-permute-start.2 = (bf16[18,768]{1,0:T(8,128)(2,1)S(1)}, bf16[18,768]{1,0:T(8,128)(2,1)S(1)}, u32[]{:S(2)}, u32[]{:S(2)}) collective-permute-start(bf16[18,768]{1,0:T(8,128)(2,1)S(1)} %get-tuple-element.52), channel_id=1, source_target_pairs={{0,1},{1,0},{2,3},{3,2},{4,5},{5,4},{6,7},{7,6},{8,9},{9,8},{10,11... | collective-permute-start | bytes 82952 | tf_op jit(solution)/shard_map/ppermute | solution.py:41
  12.1 3.4 %collective-permute-start.3 = (bf16[18,768]{1,0:T(8,128)(2,1)S(1)}, bf16[18,768]{1,0:T(8,128)(2,1)S(1)}, u32[]{:S(2)}, u32[]{:S(2)}) collective-permute-start(bf16[18,768]{1,0:T(8,128)(2,1)S(1)} %get-tuple-element.51), channel_id=1, source_target_pairs={{0,15},{1,2},{2,1},{3,4},{4,3},{5,6},{6,5},{7,8},{8,7},{9,10},{10,... | collective-permute-start | bytes 82952 | tf_op jit(solution)/shard_map/ppermute | solution.py:42
  20.3 13.0 %copy-start.7 = (bf16[512,768]{1,0:T(8,128)(2,1)}, bf16[512,768]{1,0:T(8,128)(2,1)S(1)}, u32[]{:S(2)}) copy-start(bf16[512,768]{1,0:T(8,128)(2,1)S(1)} %get-tuple-element.20) | copy-start | bytes 2359300
  20.3 19.4 %all-to-all-start = ((bf16[16,8,768]{2,1,0:T(8,128)(2,1)}), bf16[16,8,768]{2,1,0:T(8,128)(2,1)S(1)}, u32[]{:S(2)}, u32[]{:S(2)}) async-start(bf16[16,8,768]{2,1,0:T(8,128)(2,1)} %get-tuple-element.21), calls=%async_computation | async-start | bytes 393216 | tf_op jit(solution)/shard_map/all_to_all | solution.py:490
  54.9 12.4 %collective-permute-start.10 = (bf16[1,128,384]{2,1,0:T(8,128)(2,1)}, bf16[1,128,384]{2,1,0:T(8,128)(2,1)}, u32[]{:S(2)}, u32[]{:S(2)}) collective-permute-start(bf16[1,128,384]{2,1,0:T(8,128)(2,1)} %dynamic-slice_bitcast_fusion), channel_id=1, source_target_pairs={{0,16},{16,0},{32,48},{48,32},{64,80},{80,64},{96,112},{112,96},{1... | collective-permute-start | bytes 294920 | tf_op jit(solution)/shard_map/ppermute | solution.py:495
  56.3 32.4 %collective-permute-start.8 = (bf16[768,384]{1,0:T(8,128)(2,1)}, bf16[768,384]{1,0:T(8,128)(2,1)}, u32[]{:S(2)}, u32[]{:S(2)}) collective-permute-start(bf16[768,384]{1,0:T(8,128)(2,1)} %convolution_convert_fusion.3), channel_id=1, source_target_pairs={{0,1},{1,0},{2,3},{3,2},{4,5},{5,4},{6,7},{7,6},{8,9},{9,8},{10,11... | collective-permute-start | bytes 1769480 | tf_op jit(solution)/shard_map/ppermute | solution.py:510
  56.9 31.9 %collective-permute-start.9 = (bf16[768,384]{1,0:T(8,128)(2,1)}, bf16[768,384]{1,0:T(8,128)(2,1)}, u32[]{:S(2)}, u32[]{:S(2)}) collective-permute-start(bf16[768,384]{1,0:T(8,128)(2,1)} %fusion.1), channel_id=1, source_target_pairs={{0,1},{1,0},{2,3},{3,2},{4,5},{5,4},{6,7},{7,6},{8,9},{9,8},{10,11... | collective-permute-start | bytes 1769480 | tf_op jit(solution)/shard_map/ppermute | solution.py:510
  56.9 20.3 %all-to-all-start.1 = ((bf16[16,2,8,768]{3,2,1,0:T(8,128)(2,1)}), bf16[16,2,8,768]{3,2,1,0:T(8,128)(2,1)}, u32[]{:S(2)}, u32[]{:S(2)}) async-start(bf16[16,2,8,768]{3,2,1,0:T(8,128)(2,1)} %get-tuple-element.23), calls=%async_computation.1 | async-start | bytes 786432 | tf_op jit(solution)/shard_map/all_to_all | solution.py:499
  67.3 7.2 %copy-start.19 = (f32[9,8,768]{2,1,0:T(8,128)}, f32[9,8,768]{2,1,0:T(8,128)S(1)}, u32[]{:S(2)}) copy-start(f32[9,8,768]{2,1,0:T(8,128)S(1)} %get-tuple-element.27.windows) | copy-start | bytes 663556
  67.3 8.2 %copy-start.27 = (f32[9,768]{1,0:T(8,128)}, f32[9,768]{1,0:T(8,128)S(1)}, u32[]{:S(2)}) copy-start(f32[9,768]{1,0:T(8,128)S(1)} %get-tuple-element.26.early) | copy-start | bytes 82948
  68.4 6.1 %collective-permute-start.11 = (bf16[2,128,384]{2,1,0:T(8,128)(2,1)S(1)}, bf16[2,128,384]{2,1,0:T(8,128)(2,1)S(1)}, u32[]{:S(2)}, u32[]{:S(2)}) collective-permute-start(bf16[2,128,384]{2,1,0:T(8,128)(2,1)S(1)} %pad_maximum_fusion.1), channel_id=1, source_target_pairs={{0,32},{16,48},{32,0},{48,16},{64,96},{80,112},{96,64},{112,80},{1... | collective-permute-start | bytes 589832 | tf_op jit(solution)/shard_map/ppermute | solution.py:495
  75.5 53.4 %collective-permute-start.12 = (bf16[4,128,384]{2,1,0:T(8,128)(2,1)S(1)}, bf16[4,128,384]{2,1,0:T(8,128)(2,1)}, u32[]{:S(2)}, u32[]{:S(2)}) collective-permute-start(bf16[4,128,384]{2,1,0:T(8,128)(2,1)S(1)} %pad_maximum_fusion.near), channel_id=1, source_target_pairs={{0,64},{16,80},{32,96},{48,112},{64,0},{80,16},{96,32},{112,48},{1... | collective-permute-start | bytes 1179656 | tf_op jit(solution)/shard_map/ppermute | solution.py:495
  82.2 6.5 %copy-start.3 = (bf16[768,384]{1,0:T(8,128)(2,1)S(1)}, bf16[768,384]{1,0:T(8,128)(2,1)}, u32[]{:S(2)}) copy-start(bf16[768,384]{1,0:T(8,128)(2,1)} %convolution_convert_fusion.5.own_query) | copy-start | bytes 1769476
  82.2 6.5 %copy-start.4 = (bf16[768,384]{1,0:T(8,128)(2,1)S(1)}, bf16[768,384]{1,0:T(8,128)(2,1)}, u32[]{:S(2)}) copy-start(bf16[768,384]{1,0:T(8,128)(2,1)} %fusion.own_out) | copy-start | bytes 1769476
  85.1 14.9 %collective-permute-start.4 = (bf16[32,768]{1,0:T(8,128)(2,1)}, bf16[32,768]{1,0:T(8,128)(2,1)S(1)}, u32[]{:S(2)}, u32[]{:S(2)}) collective-permute-start(bf16[32,768]{1,0:T(8,128)(2,1)} %get-tuple-element.40), channel_id=1, source_target_pairs={{0,16},{16,32},{32,48},{48,64},{64,80},{80,96},{96,112},{112,0},{1... | collective-permute-start | bytes 147464 | tf_op jit(solution)/shard_map/ppermute | solution.py:34
  86.7 13.3 %collective-permute-start.5 = (bf16[32,768]{1,0:T(8,128)(2,1)}, bf16[32,768]{1,0:T(8,128)(2,1)S(1)}, u32[]{:S(2)}, u32[]{:S(2)}) collective-permute-start(bf16[32,768]{1,0:T(8,128)(2,1)} %get-tuple-element.39), channel_id=1, source_target_pairs={{16,0},{32,16},{48,32},{64,48},{80,64},{96,80},{112,96},{0,112},{1... | collective-permute-start | bytes 147464 | tf_op jit(solution)/shard_map/ppermute | solution.py:35
  91.3 8.7 %copy-start.37 = (f32[16,1,768]{2,1,0:T(1,128)S(1)}, f32[16,1,768]{2,1,0:T(1,128)}, u32[]{:S(2)}) copy-start(f32[16,1,768]{2,1,0:T(1,128)} %get-tuple-element.37) | copy-start | bytes 147460
  91.3 8.7 %copy-start.36 = (f32[16,1,768]{2,1,0:T(1,128)S(1)}, f32[16,1,768]{2,1,0:T(1,128)}, u32[]{:S(2)}) copy-start(f32[16,1,768]{2,1,0:T(1,128)} %get-tuple-element.38) | copy-start | bytes 147460
  91.3 22.7 %all-to-all-start.2 = ((bf16[64,24,384]{2,1,0:T(8,128)(2,1)}), bf16[64,24,384]{2,1,0:T(8,128)(2,1)}, u32[]{:S(2)}, u32[]{:S(2)}) async-start(bf16[64,24,384]{2,1,0:T(8,128)(2,1)} %bitcast.65), calls=%async_computation.2 | async-start | bytes 2359296 | tf_op jit(solution)/shard_map/all_to_all | solution.py:513
  100.1 13.9 %copy-start.23 = (bf16[32,768]{1,0:T(8,128)(2,1)}, bf16[32,768]{1,0:T(8,128)(2,1)S(1)}, u32[]{:S(2)}) copy-start(bf16[32,768]{1,0:T(8,128)(2,1)S(1)} %collective-permute-done.5.bottom) | copy-start | bytes 147460
  114.0 21.6 %all-to-all-start.3 = ((bf16[128,8,128]{2,1,0:T(8,128)(2,1)}), bf16[128,8,128]{2,1,0:T(8,128)(2,1)S(1)}, u32[]{:S(2)}, u32[]{:S(2)}) async-start(bf16[128,8,128]{2,1,0:T(8,128)(2,1)} %copy-done.18), calls=%async_computation.3 | async-start | bytes 524288 | tf_op jit(solution)/shard_map/all_to_all | solution.py:523
  125.7 17.5 %collective-permute-start.6 = (bf16[18,768]{1,0:T(8,128)(2,1)}, bf16[18,768]{1,0:T(8,128)(2,1)}, u32[]{:S(2)}, u32[]{:S(2)}) collective-permute-start(bf16[18,768]{1,0:T(8,128)(2,1)} %get-tuple-element.50), channel_id=1, source_target_pairs={{0,1},{1,0},{2,3},{3,2},{4,5},{5,4},{6,7},{7,6},{8,9},{9,8},{10,11... | collective-permute-start | bytes 82952 | tf_op jit(solution)/shard_map/ppermute | solution.py:41
  126.7 16.4 %collective-permute-start.7 = (bf16[18,768]{1,0:T(8,128)(2,1)}, bf16[18,768]{1,0:T(8,128)(2,1)}, u32[]{:S(2)}, u32[]{:S(2)}) collective-permute-start(bf16[18,768]{1,0:T(8,128)(2,1)} %get-tuple-element.49), channel_id=1, source_target_pairs={{0,15},{1,2},{2,1},{3,4},{4,3},{5,6},{6,5},{7,8},{8,7},{9,10},{10,... | collective-permute-start | bytes 82952 | tf_op jit(solution)/shard_map/ppermute | solution.py:42
  128.9 15.1 %copy-start.22 = (f32[9,768]{1,0:T(8,128)S(1)}, f32[9,768]{1,0:T(8,128)}, u32[]{:S(2)}) copy-start(f32[9,768]{1,0:T(8,128)} %taps.3) | copy-start | bytes 82948
  137.7 12.5 %all-to-all-start.4 = ((bf16[16,24,384]{2,1,0:T(8,128)(2,1)}), bf16[16,24,384]{2,1,0:T(8,128)(2,1)S(1)}, u32[]{:S(2)}, u32[]{:S(2)}) async-start(bf16[16,24,384]{2,1,0:T(8,128)(2,1)} %copy-done.17), calls=%async_computation.4 | async-start | bytes 589824 | tf_op jit(solution)/shard_map/all_to_all | solution.py:541
  (24 other events, 38.9 us)

commit v3 on v2

--- a/solution.py
+++ b/solution.py
@@ -11,7 +11,7 @@
 BF = jnp.bfloat16
 F32 = jnp.float32
 LANES = 128
-WIDE = 768
+WIDE = 384
 
 FINAL = (0, 1, 2, 3, 12, 13, 14, 15)
 PARTNER = (5, 4, 7, 6, 9, 8, 11, 10)
@@ -226,12 +226,12 @@
 
 def attend(query, dout, cells, w_key, w_value):
     tokens, channels = query.shape
-    by_pair = pl.BlockSpec((tokens, 384), lambda i: (0, i))
-    turned = pl.BlockSpec((384, tokens), lambda i: (i, 0))
-    weight = pl.BlockSpec((channels, 384), lambda i: (0, i))
+    by_pair = pl.BlockSpec((tokens, 256), lambda i: (0, i))
+    turned = pl.BlockSpec((256, tokens), lambda i: (i, 0))
+    weight = pl.BlockSpec((channels, 256), lambda i: (0, i))
     return pl.pallas_call(
         attend_kernel,
-        grid=(channels // 384,),
+        grid=(channels // 256,),
         in_specs=[
             by_pair,
             by_pair,
@@ -239,7 +239,7 @@
             weight,
             weight,
         ],
-        out_specs=[turned, turned, pl.BlockSpec((16, 2, 8, 384), lambda i: (0, 0, 0, i))],
+        out_specs=[turned, turned, pl.BlockSpec((16, 2, 8, 256), lambda i: (0, 0, 0, i))],
         out_shape=[
             jax.ShapeDtypeStruct((channels, tokens), BF),
             jax.ShapeDtypeStruct((channels, tokens), BF),

time: 153 us -> 153 us (level)
  no operation moved by 1% of the time
where the time goes in v3:
time: 153 us; the launch traced here: 151 us
  starting transfers between devices  54.9 us (36%)
  waiting for transfers between devices  34.4 us (22%)
  Pallas kernels  23.4 us (15%)
  local copies, waits for them, and re-layouts  18.7 us (12%)
  matrix products  13 us (8%)
  other arithmetic  5.7 us (4%)
    unnamed x76, local copies, waits for them, and re-layouts  13.4 us
    all_to_all x1, waiting for transfers between devices, block_gradients(): lax.all_to_all(chip.reshape(64, 24, half), BOTH, 0, 0, tiled=True, axis_i...  13.2 us
    dot_general x6, matrix products, dot(): lax.dot_general(left, right, ((dims[0], dims[1]), ((), ())), preferred_el...  11.3 us
    all_to_all x1, starting transfers between devices, block_gradients(): cells = lax.all_to_all(normed, 'col', 0, 0, tiled=True)  11.3 us
    all_to_all x1, starting transfers between devices, block_gradients(): blocks = lax.all_to_all(block, BOTH, 0, 0, tiled=True)  10.3 us
    all_to_all x1, starting transfers between devices, block_gradients(): lax.all_to_all(chip.reshape(64, 24, half), BOTH, 0, 0, tiled=True, axis_i...  8.46 us
    pallas_call x1, Pallas kernels, attend(): pl.pallas_call(attend_kernel, grid=(channels // 256,), in_specs=[by_pair,...  7.05 us
    all_to_all x1, waiting for transfers between devices, block_gradients(): blocks = lax.all_to_all(block, BOTH, 0, 0, tiled=True)  6.69 us
  transfers between devices with their start and end apart: 18, of which 6 were waited for; matrix products, arithmetic and copies ran while one was open for 10% of the time, Pallas kernels for 8%

profile of v3, /device:TPU:1, one launch (start us, length us, event | category | flops | bytes accessed | tf_op | source)
XLA Modules:
  0.0 151.3 jit_solution(5519588047040654396)
XLA Ops:
  1.6 2.5 %collective-permute-start = (bf16[32,768]{1,0:T(8,128)(2,1)S(1)}, bf16[32,768]{1,0:T(8,128)(2,1)S(1)}, u32[]{:S(2)}, u32[]{:S(2)}) collective-permute-start(bf16[32,768]{1,0:T(8,128)(2,1)S(1)} %get-tuple-element.44), channel_id=1, source_target_pairs={{0,16},{16,32},{32,48},{48,64},{64,80},{80,96},{96,112},{112,0},{1... | collective-permute-start | bytes 147464 | tf_op jit(solution)/shard_map/ppermute | solution.py:34
  4.1 2.3 %collective-permute-start.1 = (bf16[32,768]{1,0:T(8,128)(2,1)S(1)}, bf16[32,768]{1,0:T(8,128)(2,1)S(1)}, u32[]{:S(2)}, u32[]{:S(2)}) collective-permute-start(bf16[32,768]{1,0:T(8,128)(2,1)S(1)} %get-tuple-element.43), channel_id=1, source_target_pairs={{16,0},{32,16},{48,32},{64,48},{80,64},{96,80},{112,96},{0,112},{1... | collective-permute-start | bytes 147464 | tf_op jit(solution)/shard_map/ppermute | solution.py:35
  7.5 3.3 %convolution_convert_fusion.dout = bf16[512,768]{1,0:T(8,128)(2,1)} fusion(bf16[512,768]{1,0:T(8,128)(2,1)} %bitcast.66, bf16[768,768]{1,0:T(8,128)(2,1)} %param.12), kind=kOutput, calls=%fused_computation.1 | convolution fusion | flops 604372992 | bytes 2752512 | tf_op jit(solution)/shard_map/dot_general | solution.py:57
  12.1 1.3 collective-permute-start.3
  13.5 2.0 %collective-permute-done.3 = bf16[18,768]{1,0:T(8,128)(2,1)S(1)} collective-permute-done((bf16[18,768]{1,0:T(8,128)(2,1)S(1)}, bf16[18,768]{1,0:T(8,128)(2,1)S(1)}, u32[]{:S(2)}, u32[]{:S(2)}) %collective-permute-start.3) | collective-permute-done | bytes 27680 | tf_op jit(solution)/shard_map/ppermute | solution.py:42
  15.6 3.7 %mix.1 = (bf16[512,768]{1,0:T(8,128)(2,1)S(1)}, f32[8,768]{1,0:T(8,128)S(1)}, f32[8,128]{1,0:T(8,128)S(1)}, bf16[16,8,768]{2,1,0:T(8,128)(2,1)}) custom-call(s32[6]{0:T(128)S(1)} %pad_add_fusion.flags, bf16[16,32,768]{2,1,0:T(8,128)(2,1)S(1)} %copy-done.2, bf16[32,768]{1,0:T(8,128)(2,1)S(1)} %collective-permute-done.top, ...), custom_call_target="tpu_custom_call" | custom-call | flops 8000000 | bytes 2000000 | tf_op jit(solution)/shard_map/mix/pallas_call | solution.py:147
  20.5 11.3 %all-to-all-start = ((bf16[16,8,768]{2,1,0:T(8,128)(2,1)}), bf16[16,8,768]{2,1,0:T(8,128)(2,1)S(1)}, u32[]{:S(2)}, u32[]{:S(2)}) async-start(bf16[16,8,768]{2,1,0:T(8,128)(2,1)} %get-tuple-element.21), calls=%async_computation | async-start | bytes 393216 | tf_op jit(solution)/shard_map/all_to_all | solution.py:490
  31.8 1.7 %convolution_convert_fusion.1.query = bf16[512,768]{1,0:T(8,128)(2,1)} fusion(bf16[512,768]{1,0:T(8,128)(2,1)S(1)} %get-tuple-element.20, bf16[768,768]{1,0:T(8,128)(2,1)S(1)} %copy-done), kind=kOutput, calls=%fused_computation.2 | convolution fusion | flops 604372992 | bytes 2752512 | tf_op jit(solution)/shard_map/dot_general | solution.py:492
  33.4 6.4 %all-to-all-done = bf16[16,8,768]{2,1,0:T(8,128)(2,1)S(1)} async-done(((bf16[16,8,768]{2,1,0:T(8,128)(2,1)}), bf16[16,8,768]{2,1,0:T(8,128)(2,1)S(1)}, u32[]{:S(2)}, u32[]{:S(2)}) %all-to-all-start) | async-done | bytes 196640 | tf_op jit(solution)/shard_map/all_to_all | solution.py:490
  40.6 7.0 %attend.1 = (bf16[768,512]{1,0:T(8,128)(2,1)}, bf16[768,512]{1,0:T(8,128)(2,1)}, bf16[16,2,8,768]{3,2,1,0:T(8,128)(2,1)}) custom-call(bf16[512,768]{1,0:T(8,128)(2,1)} %convolution_convert_fusion.1.query, bf16[512,768]{1,0:T(8,128)(2,1)} %convolution_convert_fusion.dout, bf16[128,768]{1,0:T(8,128)(2,1)} %bitcast.72, bf16[768,768]{1,0:T(8,128)(2,1)} %w_key.3, ...), custom_call_target="tpu_custom_call" | custom-call | flops 3000000000 | bytes 6000000 | tf_op jit(solution)/shard_map/attend/pallas_call | solution.py:232
  47.6 2.3 %convert_add_fusion = f32[512,768]{1,0:T(8,128)S(1)} fusion(bf16[512,768]{1,0:T(8,128)(2,1)} %bitcast.67, bf16[768,512]{1,0:T(8,128)(2,1)} %get-tuple-element.22, bf16[768,768]{1,0:T(8,128)(2,1)S(1)} %copy-done), kind=kOutput, calls=%fused_computation | convolution fusion | flops 604766208 | bytes 4325376 | tf_op jit(solution)/shard_map/dot_general | solution.py:57
  50.0 1.4 convolution_convert_fusion.5.own_query
  52.1 1.5 fusion.own_out
  53.5 1.4 convolution_convert_fusion.3
  54.9 1.4 fusion.1
  56.9 4.5 %all-to-all-start.1 = ((bf16[16,2,8,768]{3,2,1,0:T(8,128)(2,1)}), bf16[16,2,8,768]{3,2,1,0:T(8,128)(2,1)}, u32[]{:S(2)}, u32[]{:S(2)}) async-start(bf16[16,2,8,768]{3,2,1,0:T(8,128)(2,1)} %get-tuple-element.23), calls=%async_computation.1 | async-start | bytes 786432 | tf_op jit(solution)/shard_map/all_to_all | solution.py:499
  64.5 2.9 %tap_terms.1 = (f32[9,768]{1,0:T(8,128)S(1)}, f32[9,8,768]{2,1,0:T(8,128)S(1)}) custom-call(s32[6]{0:T(128)S(1)} %pad_add_fusion.flags, bf16[16,32,768]{2,1,0:T(8,128)(2,1)S(1)} %copy-done.2, bf16[32,768]{1,0:T(8,128)(2,1)S(1)} %copy-done.10, bf16[32,768]{1,0:T(8,128)(2,1)S(1)} %copy-done.12, bf16[18,768]{1,0:T(8,128)(2,1)S(1)} %copy-done.16, ...), custom_call_target="tpu_custom_call" | custom-call | flops 8000000 | bytes 3000000 | tf_op jit(solution)/shard_map/tap_terms/pallas_call | solution.py:309
  69.4 5.4 %collective-permute-done.11 = bf16[2,128,384]{2,1,0:T(8,128)(2,1)S(1)} collective-permute-done((bf16[2,128,384]{2,1,0:T(8,128)(2,1)S(1)}, bf16[2,128,384]{2,1,0:T(8,128)(2,1)S(1)}, u32[]{:S(2)}, u32[]{:S(2)}) %collective-permute-start.11) | collective-permute-done | bytes 196640 | tf_op jit(solution)/shard_map/ppermute | solution.py:495
  75.7 1.9 %collective-permute-start.12 = (bf16[4,128,384]{2,1,0:T(8,128)(2,1)S(1)}, bf16[4,128,384]{2,1,0:T(8,128)(2,1)}, u32[]{:S(2)}, u32[]{:S(2)}) collective-permute-start(bf16[4,128,384]{2,1,0:T(8,128)(2,1)S(1)} %pad_maximum_fusion.near), channel_id=1, source_target_pairs={{0,64},{16,80},{32,96},{48,112},{64,0},{80,16},{96,32},{112,48},{1... | collective-permute-start | bytes 1179656 | tf_op jit(solution)/shard_map/ppermute | solution.py:495
  77.6 1.3 copy-done.5
  82.6 2.2 %at_cells.1 = (f32[8,768]{1,0:T(8,128)S(1)}, bf16[128,8,128]{2,1,0:T(8,128)(2,1)S(1)}) custom-call(bf16[16,2,8,768]{3,2,1,0:T(8,128)(2,1)} %all-to-all-done.1.terms, bf16[768,768]{1,0:T(8,128)(2,1)S(1)} %copy-done.5, bf16[768,768]{1,0:T(8,128)(2,1)S(1)} %copy-done.6, f32[8,768]{1,0:T(8,128)S(1)} %copy-done.30, f32[8,128]{1,0:T(8,128)S(1)} %get-tuple-element.25.inverse, ...), custom_call_target="tpu_custom_call" | custom-call | flops 30000000 | bytes 3500000 | tf_op jit(solution)/shard_map/at_cells/pallas_call | solution.py:366
  85.5 1.6 %collective-permute-start.4 = (bf16[32,768]{1,0:T(8,128)(2,1)}, bf16[32,768]{1,0:T(8,128)(2,1)S(1)}, u32[]{:S(2)}, u32[]{:S(2)}) collective-permute-start(bf16[32,768]{1,0:T(8,128)(2,1)} %get-tuple-element.40), channel_id=1, source_target_pairs={{0,16},{16,32},{32,48},{48,64},{64,80},{80,96},{96,112},{112,0},{1... | collective-permute-start | bytes 147464 | tf_op jit(solution)/shard_map/ppermute | solution.py:34
  87.2 2.0 %collective-permute-start.5 = (bf16[32,768]{1,0:T(8,128)(2,1)}, bf16[32,768]{1,0:T(8,128)(2,1)S(1)}, u32[]{:S(2)}, u32[]{:S(2)}) collective-permute-start(bf16[32,768]{1,0:T(8,128)(2,1)} %get-tuple-element.39), channel_id=1, source_target_pairs={{16,0},{32,16},{48,32},{64,48},{80,64},{96,80},{112,96},{0,112},{1... | collective-permute-start | bytes 147464 | tf_op jit(solution)/shard_map/ppermute | solution.py:35
  89.2 1.5 chip_sums.1
  91.8 8.5 %all-to-all-start.2 = ((bf16[64,24,384]{2,1,0:T(8,128)(2,1)}), bf16[64,24,384]{2,1,0:T(8,128)(2,1)}, u32[]{:S(2)}, u32[]{:S(2)}) async-start(bf16[64,24,384]{2,1,0:T(8,128)(2,1)} %bitcast.65), calls=%async_computation.2 | async-start | bytes 2359296 | tf_op jit(solution)/shard_map/all_to_all | solution.py:513
  101.0 13.2 %all-to-all-done.2.got = bf16[64,24,384]{2,1,0:T(8,128)(2,1)} async-done(((bf16[64,24,384]{2,1,0:T(8,128)(2,1)}), bf16[64,24,384]{2,1,0:T(8,128)(2,1)}, u32[]{:S(2)}, u32[]{:S(2)}) %all-to-all-start.2) | async-done | bytes 1179680 | tf_op jit(solution)/shard_map/all_to_all | solution.py:513
  114.3 10.3 %all-to-all-start.3 = ((bf16[128,8,128]{2,1,0:T(8,128)(2,1)}), bf16[128,8,128]{2,1,0:T(8,128)(2,1)S(1)}, u32[]{:S(2)}, u32[]{:S(2)}) async-start(bf16[128,8,128]{2,1,0:T(8,128)(2,1)} %copy-done.18), calls=%async_computation.3 | async-start | bytes 524288 | tf_op jit(solution)/shard_map/all_to_all | solution.py:523
  127.7 1.5 summed.1.own
  129.1 6.7 %all-to-all-done.3.blocks = bf16[128,8,128]{2,1,0:T(8,128)(2,1)S(1)} async-done(((bf16[128,8,128]{2,1,0:T(8,128)(2,1)}), bf16[128,8,128]{2,1,0:T(8,128)(2,1)S(1)}, u32[]{:S(2)}, u32[]{:S(2)}) %all-to-all-start.3) | async-done | bytes 262176 | tf_op jit(solution)/shard_map/all_to_all | solution.py:523
  135.8 1.4 pieces.1
  138.0 5.4 %all-to-all-start.4 = ((bf16[16,24,384]{2,1,0:T(8,128)(2,1)}), bf16[16,24,384]{2,1,0:T(8,128)(2,1)S(1)}, u32[]{:S(2)}, u32[]{:S(2)}) async-start(bf16[16,24,384]{2,1,0:T(8,128)(2,1)} %copy-done.17), calls=%async_computation.4 | async-start | bytes 589824 | tf_op jit(solution)/shard_map/all_to_all | solution.py:541
  145.7 3.3 %unmix.1 = bf16[16,32,768]{2,1,0:T(8,128)(2,1)} custom-call(s32[6]{0:T(128)S(1)} %pad_add_fusion.flags, f32[16,32,768]{2,1,0:T(8,128)S(1)} %bitcast.64, f32[8,768]{1,0:T(8,128)S(1)} %copy-done.26, bf16[32,768]{1,0:T(8,128)(2,1)S(1)} %collective-permute-done.4.top, bf16[32,768]{1,0:T(8,128)(2,1)S(1)} %copy-done.24, ...), custom_call_target="tpu_custom_call" | custom-call | flops 8000000 | bytes 3000000 | tf_op jit(solution)/shard_map/unmix/pallas_call | solution.py:450
  (129 shorter events, 27.3 us)
Async XLA Ops:
  0.6 31.1 %copy-start = (bf16[768,768]{1,0:T(8,128)(2,1)S(1)}, bf16[768,768]{1,0:T(8,128)(2,1)}, u32[]{:S(2)}) copy-start(bf16[768,768]{1,0:T(8,128)(2,1)} %param.9) | copy-start | bytes 3538948
  1.6 9.4 %collective-permute-start = (bf16[32,768]{1,0:T(8,128)(2,1)S(1)}, bf16[32,768]{1,0:T(8,128)(2,1)S(1)}, u32[]{:S(2)}, u32[]{:S(2)}) collective-permute-start(bf16[32,768]{1,0:T(8,128)(2,1)S(1)} %get-tuple-element.44), channel_id=1, source_target_pairs={{0,16},{16,32},{32,48},{48,64},{64,80},{80,96},{96,112},{112,0},{1... | collective-permute-start | bytes 147464 | tf_op jit(solution)/shard_map/ppermute | solution.py:34
  4.1 6.9 %collective-permute-start.1 = (bf16[32,768]{1,0:T(8,128)(2,1)S(1)}, bf16[32,768]{1,0:T(8,128)(2,1)S(1)}, u32[]{:S(2)}, u32[]{:S(2)}) collective-permute-start(bf16[32,768]{1,0:T(8,128)(2,1)S(1)} %get-tuple-element.43), channel_id=1, source_target_pairs={{16,0},{32,16},{48,32},{64,48},{80,64},{96,80},{112,96},{0,112},{1... | collective-permute-start | bytes 147464 | tf_op jit(solution)/shard_map/ppermute | solution.py:35
  7.5 8.1 %copy-start.2 = (bf16[16,32,768]{2,1,0:T(8,128)(2,1)S(1)}, bf16[16,32,768]{2,1,0:T(8,128)(2,1)}, u32[]{:S(2)}) copy-start(bf16[16,32,768]{2,1,0:T(8,128)(2,1)} %image.3) | copy-start | bytes 2359300
  7.5 8.1 %copy-start.21 = (f32[9,768]{1,0:T(8,128)S(1)}, f32[9,768]{1,0:T(8,128)}, u32[]{:S(2)}) copy-start(f32[9,768]{1,0:T(8,128)} %taps.3) | copy-start | bytes 82948
  11.0 22.5 %copy-start.9 = (bf16[32,768]{1,0:T(8,128)(2,1)}, bf16[32,768]{1,0:T(8,128)(2,1)S(1)}, u32[]{:S(2)}) copy-start(bf16[32,768]{1,0:T(8,128)(2,1)S(1)} %collective-permute-done.top) | copy-start | bytes 147460
  11.0 22.4 %copy-start.11 = (bf16[32,768]{1,0:T(8,128)(2,1)}, bf16[32,768]{1,0:T(8,128)(2,1)S(1)}, u32[]{:S(2)}) copy-start(bf16[32,768]{1,0:T(8,128)(2,1)S(1)} %collective-permute-done.1.bottom) | copy-start | bytes 147460
  11.1 2.4 %collective-permute-start.2 = (bf16[18,768]{1,0:T(8,128)(2,1)S(1)}, bf16[18,768]{1,0:T(8,128)(2,1)S(1)}, u32[]{:S(2)}, u32[]{:S(2)}) collective-permute-start(bf16[18,768]{1,0:T(8,128)(2,1)S(1)} %get-tuple-element.52), channel_id=1, source_target_pairs={{0,1},{1,0},{2,3},{3,2},{4,5},{5,4},{6,7},{7,6},{8,9},{9,8},{10,11... | collective-permute-start | bytes 82952 | tf_op jit(solution)/shard_map/ppermute | solution.py:41
  12.1 3.4 %collective-permute-start.3 = (bf16[18,768]{1,0:T(8,128)(2,1)S(1)}, bf16[18,768]{1,0:T(8,128)(2,1)S(1)}, u32[]{:S(2)}, u32[]{:S(2)}) collective-permute-start(bf16[18,768]{1,0:T(8,128)(2,1)S(1)} %get-tuple-element.51), channel_id=1, source_target_pairs={{0,15},{1,2},{2,1},{3,4},{4,3},{5,6},{6,5},{7,8},{8,7},{9,10},{10,... | collective-permute-start | bytes 82952 | tf_op jit(solution)/shard_map/ppermute | solution.py:42
  20.5 13.0 %copy-start.7 = (bf16[512,768]{1,0:T(8,128)(2,1)}, bf16[512,768]{1,0:T(8,128)(2,1)S(1)}, u32[]{:S(2)}) copy-start(bf16[512,768]{1,0:T(8,128)(2,1)S(1)} %get-tuple-element.20) | copy-start | bytes 2359300
  20.5 19.4 %all-to-all-start = ((bf16[16,8,768]{2,1,0:T(8,128)(2,1)}), bf16[16,8,768]{2,1,0:T(8,128)(2,1)S(1)}, u32[]{:S(2)}, u32[]{:S(2)}) async-start(bf16[16,8,768]{2,1,0:T(8,128)(2,1)} %get-tuple-element.21), calls=%async_computation | async-start | bytes 393216 | tf_op jit(solution)/shard_map/all_to_all | solution.py:490
  54.9 12.5 %collective-permute-start.10 = (bf16[1,128,384]{2,1,0:T(8,128)(2,1)}, bf16[1,128,384]{2,1,0:T(8,128)(2,1)}, u32[]{:S(2)}, u32[]{:S(2)}) collective-permute-start(bf16[1,128,384]{2,1,0:T(8,128)(2,1)} %dynamic-slice_bitcast_fusion), channel_id=1, source_target_pairs={{0,16},{16,0},{32,48},{48,32},{64,80},{80,64},{96,112},{112,96},{1... | collective-permute-start | bytes 294920 | tf_op jit(solution)/shard_map/ppermute | solution.py:495
  56.4 32.8 %collective-permute-start.8 = (bf16[768,384]{1,0:T(8,128)(2,1)}, bf16[768,384]{1,0:T(8,128)(2,1)}, u32[]{:S(2)}, u32[]{:S(2)}) collective-permute-start(bf16[768,384]{1,0:T(8,128)(2,1)} %convolution_convert_fusion.3), channel_id=1, source_target_pairs={{0,1},{1,0},{2,3},{3,2},{4,5},{5,4},{6,7},{7,6},{8,9},{9,8},{10,11... | collective-permute-start | bytes 1769480 | tf_op jit(solution)/shard_map/ppermute | solution.py:510
  56.9 32.3 %collective-permute-start.9 = (bf16[768,384]{1,0:T(8,128)(2,1)}, bf16[768,384]{1,0:T(8,128)(2,1)}, u32[]{:S(2)}, u32[]{:S(2)}) collective-permute-start(bf16[768,384]{1,0:T(8,128)(2,1)} %fusion.1), channel_id=1, source_target_pairs={{0,1},{1,0},{2,3},{3,2},{4,5},{5,4},{6,7},{7,6},{8,9},{9,8},{10,11... | collective-permute-start | bytes 1769480 | tf_op jit(solution)/shard_map/ppermute | solution.py:510
  56.9 20.7 %all-to-all-start.1 = ((bf16[16,2,8,768]{3,2,1,0:T(8,128)(2,1)}), bf16[16,2,8,768]{3,2,1,0:T(8,128)(2,1)}, u32[]{:S(2)}, u32[]{:S(2)}) async-start(bf16[16,2,8,768]{3,2,1,0:T(8,128)(2,1)} %get-tuple-element.23), calls=%async_computation.1 | async-start | bytes 786432 | tf_op jit(solution)/shard_map/all_to_all | solution.py:499
  67.4 7.4 %copy-start.19 = (f32[9,8,768]{2,1,0:T(8,128)}, f32[9,8,768]{2,1,0:T(8,128)S(1)}, u32[]{:S(2)}) copy-start(f32[9,8,768]{2,1,0:T(8,128)S(1)} %get-tuple-element.27.windows) | copy-start | bytes 663556
  67.4 8.3 %copy-start.27 = (f32[9,768]{1,0:T(8,128)}, f32[9,768]{1,0:T(8,128)S(1)}, u32[]{:S(2)}) copy-start(f32[9,768]{1,0:T(8,128)S(1)} %get-tuple-element.26.early) | copy-start | bytes 82948
  68.4 6.3 %collective-permute-start.11 = (bf16[2,128,384]{2,1,0:T(8,128)(2,1)S(1)}, bf16[2,128,384]{2,1,0:T(8,128)(2,1)S(1)}, u32[]{:S(2)}, u32[]{:S(2)}) collective-permute-start(bf16[2,128,384]{2,1,0:T(8,128)(2,1)S(1)} %pad_maximum_fusion.1), channel_id=1, source_target_pairs={{0,32},{16,48},{32,0},{48,16},{64,96},{80,112},{96,64},{112,80},{1... | collective-permute-start | bytes 589832 | tf_op jit(solution)/shard_map/ppermute | solution.py:495
  75.7 53.4 %collective-permute-start.12 = (bf16[4,128,384]{2,1,0:T(8,128)(2,1)S(1)}, bf16[4,128,384]{2,1,0:T(8,128)(2,1)}, u32[]{:S(2)}, u32[]{:S(2)}) collective-permute-start(bf16[4,128,384]{2,1,0:T(8,128)(2,1)S(1)} %pad_maximum_fusion.near), channel_id=1, source_target_pairs={{0,64},{16,80},{32,96},{48,112},{64,0},{80,16},{96,32},{112,48},{1... | collective-permute-start | bytes 1179656 | tf_op jit(solution)/shard_map/ppermute | solution.py:495
  82.6 6.5 %copy-start.3 = (bf16[768,384]{1,0:T(8,128)(2,1)S(1)}, bf16[768,384]{1,0:T(8,128)(2,1)}, u32[]{:S(2)}) copy-start(bf16[768,384]{1,0:T(8,128)(2,1)} %convolution_convert_fusion.5.own_query) | copy-start | bytes 1769476
  82.6 6.5 %copy-start.4 = (bf16[768,384]{1,0:T(8,128)(2,1)S(1)}, bf16[768,384]{1,0:T(8,128)(2,1)}, u32[]{:S(2)}) copy-start(bf16[768,384]{1,0:T(8,128)(2,1)} %fusion.own_out) | copy-start | bytes 1769476
  85.5 14.8 %collective-permute-start.4 = (bf16[32,768]{1,0:T(8,128)(2,1)}, bf16[32,768]{1,0:T(8,128)(2,1)S(1)}, u32[]{:S(2)}, u32[]{:S(2)}) collective-permute-start(bf16[32,768]{1,0:T(8,128)(2,1)} %get-tuple-element.40), channel_id=1, source_target_pairs={{0,16},{16,32},{32,48},{48,64},{64,80},{80,96},{96,112},{112,0},{1... | collective-permute-start | bytes 147464 | tf_op jit(solution)/shard_map/ppermute | solution.py:34
  87.2 13.2 %collective-permute-start.5 = (bf16[32,768]{1,0:T(8,128)(2,1)}, bf16[32,768]{1,0:T(8,128)(2,1)S(1)}, u32[]{:S(2)}, u32[]{:S(2)}) collective-permute-start(bf16[32,768]{1,0:T(8,128)(2,1)} %get-tuple-element.39), channel_id=1, source_target_pairs={{16,0},{32,16},{48,32},{64,48},{80,64},{96,80},{112,96},{0,112},{1... | collective-permute-start | bytes 147464 | tf_op jit(solution)/shard_map/ppermute | solution.py:35
  91.8 8.5 %copy-start.37 = (f32[16,1,768]{2,1,0:T(1,128)S(1)}, f32[16,1,768]{2,1,0:T(1,128)}, u32[]{:S(2)}) copy-start(f32[16,1,768]{2,1,0:T(1,128)} %get-tuple-element.37) | copy-start | bytes 147460
  91.8 8.5 %copy-start.36 = (f32[16,1,768]{2,1,0:T(1,128)S(1)}, f32[16,1,768]{2,1,0:T(1,128)}, u32[]{:S(2)}) copy-start(f32[16,1,768]{2,1,0:T(1,128)} %get-tuple-element.38) | copy-start | bytes 147460
  91.8 22.5 %all-to-all-start.2 = ((bf16[64,24,384]{2,1,0:T(8,128)(2,1)}), bf16[64,24,384]{2,1,0:T(8,128)(2,1)}, u32[]{:S(2)}, u32[]{:S(2)}) async-start(bf16[64,24,384]{2,1,0:T(8,128)(2,1)} %bitcast.65), calls=%async_computation.2 | async-start | bytes 2359296 | tf_op jit(solution)/shard_map/all_to_all | solution.py:513
  100.3 13.9 %copy-start.23 = (bf16[32,768]{1,0:T(8,128)(2,1)}, bf16[32,768]{1,0:T(8,128)(2,1)S(1)}, u32[]{:S(2)}) copy-start(bf16[32,768]{1,0:T(8,128)(2,1)S(1)} %collective-permute-done.5.bottom) | copy-start | bytes 147460
  114.3 21.6 %all-to-all-start.3 = ((bf16[128,8,128]{2,1,0:T(8,128)(2,1)}), bf16[128,8,128]{2,1,0:T(8,128)(2,1)S(1)}, u32[]{:S(2)}, u32[]{:S(2)}) async-start(bf16[128,8,128]{2,1,0:T(8,128)(2,1)} %copy-done.18), calls=%async_computation.3 | async-start | bytes 524288 | tf_op jit(solution)/shard_map/all_to_all | solution.py:523
  125.9 17.5 %collective-permute-start.6 = (bf16[18,768]{1,0:T(8,128)(2,1)}, bf16[18,768]{1,0:T(8,128)(2,1)}, u32[]{:S(2)}, u32[]{:S(2)}) collective-permute-start(bf16[18,768]{1,0:T(8,128)(2,1)} %get-tuple-element.50), channel_id=1, source_target_pairs={{0,1},{1,0},{2,3},{3,2},{4,5},{5,4},{6,7},{7,6},{8,9},{9,8},{10,11... | collective-permute-start | bytes 82952 | tf_op jit(solution)/shard_map/ppermute | solution.py:41
  127.0 16.4 %collective-permute-start.7 = (bf16[18,768]{1,0:T(8,128)(2,1)}, bf16[18,768]{1,0:T(8,128)(2,1)}, u32[]{:S(2)}, u32[]{:S(2)}) collective-permute-start(bf16[18,768]{1,0:T(8,128)(2,1)} %get-tuple-element.49), channel_id=1, source_target_pairs={{0,15},{1,2},{2,1},{3,4},{4,3},{5,6},{6,5},{7,8},{8,7},{9,10},{10,... | collective-permute-start | bytes 82952 | tf_op jit(solution)/shard_map/ppermute | solution.py:42
  129.1 15.1 %copy-start.22 = (f32[9,768]{1,0:T(8,128)S(1)}, f32[9,768]{1,0:T(8,128)}, u32[]{:S(2)}) copy-start(f32[9,768]{1,0:T(8,128)} %taps.3) | copy-start | bytes 82948
  138.0 12.5 %all-to-all-start.4 = ((bf16[16,24,384]{2,1,0:T(8,128)(2,1)}), bf16[16,24,384]{2,1,0:T(8,128)(2,1)S(1)}, u32[]{:S(2)}, u32[]{:S(2)}) async-start(bf16[16,24,384]{2,1,0:T(8,128)(2,1)} %copy-done.17), calls=%async_computation.4 | async-start | bytes 589824 | tf_op jit(solution)/shard_map/all_to_all | solution.py:541
  (24 other events, 39.1 us)
